TPU v7x, 32 devices: a whole 2x2x4 slice. The times are simulated.
32 devices in a mesh: ka: 16 (over z, x, core), mu: 2 (over y).
Axes of the slice: x: 2, y: 2, z: 4, core: 2. Of those that a mesh axis runs over, the one named last changes fastest.
Arguments:
- vectors: float32 [3, 16, 4096], P(None, 'ka', 'mu'), may hold values from -6 to 6
- phi_val: bfloat16 [16, 64, 2048], P('ka', None, 'mu'), may hold values from -6 to 6
- phi_con: bfloat16 [16, 64, 2048], P('ka', None, 'mu'), may hold values from -6 to 6
- screened: bfloat16 [4, 2048, 2048], P(None, 'mu'), may hold values from -4.5776367e-05 to 4.5776367e-05
- partner: int32 [16, 4], P('ka'), may hold values from 0 to 15, as said below
Outputs:
- result: float32 [3, 16, 4096], P(None, 'ka', 'mu')
Inputs may be any that keep to these rules, and one draw needn't show every extreme that they name: With s = (1, -1, 2, -2) for offsets 0 to 3, partner[k, o] = (k - s[o]) modulo 16; each ka index j holds exactly one k-point, k-point j.
All inputs are finite; a program needn't handle non-finite values.
Results may differ from a plain program's by a relative error of at most 0.0058.
Values may be sent and summed in bfloat16 or wider, within the bound.
No kernel may reach another device: no remote copies, remote signals or barrier semaphores. Data moves between devices by JAX's collectives and lax.ppermute only.
A program may use at most 64 MiB of HBM per device.

v0:
```python
import jax
import jax.numpy as jnp
from jax import lax
from jax.sharding import PartitionSpec as P

cycle_steps = (1, -1, 2, -2)


def passed_along(value, axis, steps):
    count = lax.axis_size(axis)
    pairs = [(source, (source + steps) % count) for source in range(count)]
    return lax.ppermute(value, axis, pairs)


def local(vectors, phi_val, phi_con, screened, partner):
    local_points = phi_val.shape[0]
    vec_count = vectors.shape[0]
    valence = phi_val.shape[1]
    conduction = phi_con.shape[1]
    vec_coded = vectors.astype(jnp.bfloat16)
    con_home, vec_home = (
        lax.all_gather(phi_con, "mu", axis=2, tiled=True),
        lax.all_gather(vec_coded, "mu", axis=2, tiled=True),
    )
    running_sum = jnp.zeros((vec_count, local_points, valence, conduction), jnp.float32)
    for offset, cycle_step in enumerate(cycle_steps):
        val_far, con_far, vec_far = passed_along((phi_val, con_home, vec_home), "ka", cycle_step)
        slot_index = partner[:, offset] % local_points
        val_sel = jnp.take(val_far, slot_index, axis=0)
        con_sel = jnp.take(con_far, slot_index, axis=0)
        vec_sel = jnp.take(vec_far, slot_index, axis=1).reshape(
            vec_count, local_points, valence, conduction
        )
        kernel = screened[offset]

        def per_vector(vec_single):
            blended = jnp.einsum(
                "kvc,kcn->kvn", vec_single, con_sel, preferred_element_type=jnp.float32
            ).astype(jnp.bfloat16)
            paired = jnp.einsum(
                "kvm,kvn->kmn", val_sel, blended, preferred_element_type=jnp.float32
            )
            weighted = (kernel.astype(jnp.float32)[None] * paired).astype(jnp.bfloat16)
            folded = jnp.einsum(
                "kmn,kcn->kmc", weighted, con_home, preferred_element_type=jnp.float32
            ).astype(jnp.bfloat16)
            return jnp.einsum("kvm,kmc->kvc", phi_val, folded, preferred_element_type=jnp.float32)

        running_sum = running_sum + lax.map(per_vector, vec_sel)
    pair_terms = running_sum.reshape(vec_count, local_points, valence * conduction)
    return lax.psum_scatter(pair_terms, "mu", scatter_dimension=2, tiled=True)


def solution(mesh):
    placed = (
        P(None, "ka", "mu"),
        P("ka", None, "mu"),
        P("ka", None, "mu"),
        P(None, "mu", None),
        P("ka", None),
    )
    return jax.shard_map(
        local, mesh=mesh, in_specs=placed, out_specs=P(None, "ka", "mu"), check_vma=False
    )
```

profile of v0, /device:TPU:0, one launch (start us, length us, event | category | flops | bytes accessed | tf_op | source)
XLA Modules:
  0.0 188.7 jit_solution(10039181478914680342)
XLA Ops:
  6.5 0.8 convert_element_type.63
  7.3 5.5 %all_gather.6 = bf16[3,1,4096]{2,1,0:T(2,128)(2,1)S(1)} all-gather(bf16[3,1,2048]{2,1,0:T(2,128)(2,1)S(1)} %convert_element_type.63), channel_id=1, replica_groups=mesh['ka'=16,'mu'=2] {'mu'}, dimensions={2}, use_global_device_ids=true | all-gather | bytes 36864 | tf_op jit(solution)/shard_map/all_gather | solution.py:23
  12.8 4.4 %collective-permute-start.3 = (bf16[3,1,4096]{2,1,0:T(2,128)(2,1)S(1)}, bf16[3,1,4096]{2,1,0:T(2,128)(2,1)S(1)}, u32[]{:S(2)}, u32[]{:S(2)}) collective-permute-start(bf16[3,1,4096]{2,1,0:T(2,128)(2,1)S(1)} %all_gather.6), channel_id=1, source_target_pairs={{0,30},{2,0},{4,2},{6,4},{8,6},{10,8},{12,10},{14,12},{16,14},{18,... | collective-permute-start | bytes 73736 | tf_op jit(solution)/shard_map/ppermute | solution.py:12
  17.2 4.7 %collective-permute-start.9 = (bf16[3,1,4096]{2,1,0:T(2,128)(2,1)S(1)}, bf16[3,1,4096]{2,1,0:T(2,128)(2,1)S(1)}, u32[]{:S(2)}, u32[]{:S(2)}) collective-permute-start(bf16[3,1,4096]{2,1,0:T(2,128)(2,1)S(1)} %all_gather.6), channel_id=1, source_target_pairs={{0,28},{2,30},{4,0},{6,2},{8,4},{10,6},{12,8},{14,10},{16,12},{18,... | collective-permute-start | bytes 73736 | tf_op jit(solution)/shard_map/ppermute | solution.py:12
  21.9 7.5 %all_gather.7 = bf16[1,64,2048]{2,1,0:T(8,128)(2,1)} all-gather(bf16[1,64,1024]{2,1,0:T(8,128)(2,1)} %param.15), channel_id=1, replica_groups=mesh['ka'=16,'mu'=2] {'mu'}, dimensions={2}, use_global_device_ids=true | all-gather | bytes 393216 | tf_op jit(solution)/shard_map/all_gather | solution.py:22
  29.4 12.4 %slice_bitcast_fusion.2 = (bf16[1024,2048]{1,0:T(8,128)(2,1)}, bf16[1024,2048]{1,0:T(8,128)(2,1)}, bf16[1024,2048]{1,0:T(8,128)(2,1)}, bf16[1024,2048]{1,0:T(8,128)(2,1)}) fusion(bf16[4,1024,2048]{2,1,0:T(8,128)(2,1)} %param.16), kind=kLoop, calls=%fused_computation.60 | loop fusion | bytes 33554432 | tf_op jit(solution)/shard_map/squeeze | solution.py:34
  41.8 0.1 reduce
  42.0 0.1 gather.48
  42.1 4.5 %collective-permute-start.4 = (bf16[1,64,2048]{2,1,0:T(8,128)(2,1)}, bf16[1,64,2048]{2,1,0:T(8,128)(2,1)S(1)}, u32[]{:S(2)}, u32[]{:S(2)}) collective-permute-start(bf16[1,64,2048]{2,1,0:T(8,128)(2,1)} %all_gather.7), channel_id=1, source_target_pairs={{0,30},{2,0},{4,2},{6,4},{8,6},{10,8},{12,10},{14,12},{16,14},{18,... | collective-permute-start | bytes 786440 | tf_op jit(solution)/shard_map/ppermute | solution.py:12
  46.6 0.1 reduce.1
  46.7 0.1 gather.52
  46.8 0.5 collective-permute-start.5
  47.4 0.1 reduce.2
  47.5 0.1 gather.56
  47.7 0.1 reduce.3
  47.9 0.1 gather.60
  48.1 4.8 %collective-permute-start.10 = (bf16[1,64,2048]{2,1,0:T(8,128)(2,1)}, bf16[1,64,2048]{2,1,0:T(8,128)(2,1)S(1)}, u32[]{:S(2)}, u32[]{:S(2)}) collective-permute-start(bf16[1,64,2048]{2,1,0:T(8,128)(2,1)} %all_gather.7), channel_id=1, source_target_pairs={{0,28},{2,30},{4,0},{6,2},{8,4},{10,6},{12,8},{14,10},{16,12},{18,... | collective-permute-start | bytes 786440 | tf_op jit(solution)/shard_map/ppermute | solution.py:12
  52.8 18.3 %while.40 = (s32[]{:T(128)}, f32[3,1,64,64]{2,3,1,0:T(8,128)S(1)}, bf16[1024,2048]{1,0:T(8,128)(2,1)}, bf16[3,1,64,64]{3,2,1,0:T(8,128)(2,1)S(1)}, bf16[1,64,204...) while((s32[]{:T(128)}, f32[3,1,64,64]{2,3,1,0:T(8,128)S(1)}, ...), condition=%wide.region_1.2_spmd, body=%wide.region_0.1_spmd.sunk | while | flops 568524800 | bytes 5947493 | solution.py:49
  52.8 0.2 convolution_convert_fusion.8
  53.0 4.7 %fusion.99 = bf16[1024,64]{1,0:T(8,128)(2,1)S(1)} fusion(bf16[1024,2048]{1,0:T(8,128)(2,1)} %get-tuple-element.515, bf16[64,2048]{1,0:T(8,128)(2,1)S(1)} %convolution_convert_fusion.8, bf16[1,64,2048]{2,1,0:T(8,128)(2,1)} %get-tuple-element.519, bf16[1,64,1024]{2,1,0:T(8,128)(2,1)S(1)} %get-tuple-element.518), kind=kOutput, calls=%fused_computation.4.clone.1 | convolution fusion | flops 543227904 | bytes 4980736 | tf_op jit(solution)/shard_map/while/body/eval_jaxpr/kmn,kcn->kmc/dot_general | solution.py:44
  57.8 1.1 fusion.100
  58.9 0.2 convolution_convert_fusion.8
  59.1 4.7 %fusion.99 = bf16[1024,64]{1,0:T(8,128)(2,1)S(1)} fusion(bf16[1024,2048]{1,0:T(8,128)(2,1)} %get-tuple-element.515, bf16[64,2048]{1,0:T(8,128)(2,1)S(1)} %convolution_convert_fusion.8, bf16[1,64,2048]{2,1,0:T(8,128)(2,1)} %get-tuple-element.519, bf16[1,64,1024]{2,1,0:T(8,128)(2,1)S(1)} %get-tuple-element.518), kind=kOutput, calls=%fused_computation.4.clone.1 | convolution fusion | flops 543227904 | bytes 4980736 | tf_op jit(solution)/shard_map/while/body/eval_jaxpr/kmn,kcn->kmc/dot_general | solution.py:44
  63.8 1.1 fusion.100
  65.0 0.2 convolution_convert_fusion.8
  65.2 4.7 %fusion.99 = bf16[1024,64]{1,0:T(8,128)(2,1)S(1)} fusion(bf16[1024,2048]{1,0:T(8,128)(2,1)} %get-tuple-element.515, bf16[64,2048]{1,0:T(8,128)(2,1)S(1)} %convolution_convert_fusion.8, bf16[1,64,2048]{2,1,0:T(8,128)(2,1)} %get-tuple-element.519, bf16[1,64,1024]{2,1,0:T(8,128)(2,1)S(1)} %get-tuple-element.518), kind=kOutput, calls=%fused_computation.4.clone.1 | convolution fusion | flops 543227904 | bytes 4980736 | tf_op jit(solution)/shard_map/while/body/eval_jaxpr/kmn,kcn->kmc/dot_general | solution.py:44
  69.9 1.1 fusion.100
  71.1 2.2 %collective-permute-start.11 = (bf16[1,64,1024]{2,1,0:T(8,128)(2,1)}, bf16[1,64,1024]{2,1,0:T(8,128)(2,1)S(1)}, u32[]{:S(2)}, u32[]{:S(2)}) collective-permute-start(bf16[1,64,1024]{2,1,0:T(8,128)(2,1)} %param.14), channel_id=1, source_target_pairs={{0,28},{2,30},{4,0},{6,2},{8,4},{10,6},{12,8},{14,10},{16,12},{18,... | collective-permute-start | bytes 393224 | tf_op jit(solution)/shard_map/ppermute | solution.py:12
  73.3 18.3 %while.41 = (s32[]{:T(128)}, f32[3,1,64,64]{2,3,1,0:T(8,128)S(1)}, bf16[1024,2048]{1,0:T(8,128)(2,1)}, bf16[3,1,64,64]{3,2,1,0:T(8,128)(2,1)S(1)}, bf16[1,64,204...) while((s32[]{:T(128)}, f32[3,1,64,64]{2,3,1,0:T(8,128)S(1)}, ...), condition=%wide.region_3.4_spmd, body=%wide.region_2.3_spmd.sunk | while | flops 568524800 | bytes 5947493 | solution.py:49
  73.3 0.2 convolution_convert_fusion.9
  73.5 4.7 %fusion.108 = bf16[1024,64]{1,0:T(8,128)(2,1)S(1)} fusion(bf16[1024,2048]{1,0:T(8,128)(2,1)} %get-tuple-element.542, bf16[64,2048]{1,0:T(8,128)(2,1)S(1)} %convolution_convert_fusion.9, bf16[1,64,2048]{2,1,0:T(8,128)(2,1)} %get-tuple-element.546, bf16[1,64,1024]{2,1,0:T(8,128)(2,1)S(1)} %get-tuple-element.545), kind=kOutput, calls=%fused_computation.18.clone.1 | convolution fusion | flops 543227904 | bytes 4980736 | tf_op jit(solution)/shard_map/while/body/eval_jaxpr/kmn,kcn->kmc/dot_general | solution.py:44
  78.2 1.1 fusion.109
  79.4 0.2 convolution_convert_fusion.9
  79.6 4.7 %fusion.108 = bf16[1024,64]{1,0:T(8,128)(2,1)S(1)} fusion(bf16[1024,2048]{1,0:T(8,128)(2,1)} %get-tuple-element.542, bf16[64,2048]{1,0:T(8,128)(2,1)S(1)} %convolution_convert_fusion.9, bf16[1,64,2048]{2,1,0:T(8,128)(2,1)} %get-tuple-element.546, bf16[1,64,1024]{2,1,0:T(8,128)(2,1)S(1)} %get-tuple-element.545), kind=kOutput, calls=%fused_computation.18.clone.1 | convolution fusion | flops 543227904 | bytes 4980736 | tf_op jit(solution)/shard_map/while/body/eval_jaxpr/kmn,kcn->kmc/dot_general | solution.py:44
  84.3 1.1 fusion.109
  85.5 0.2 convolution_convert_fusion.9
  85.7 4.7 %fusion.108 = bf16[1024,64]{1,0:T(8,128)(2,1)S(1)} fusion(bf16[1024,2048]{1,0:T(8,128)(2,1)} %get-tuple-element.542, bf16[64,2048]{1,0:T(8,128)(2,1)S(1)} %convolution_convert_fusion.9, bf16[1,64,2048]{2,1,0:T(8,128)(2,1)} %get-tuple-element.546, bf16[1,64,1024]{2,1,0:T(8,128)(2,1)S(1)} %get-tuple-element.545), kind=kOutput, calls=%fused_computation.18.clone.1 | convolution fusion | flops 543227904 | bytes 4980736 | tf_op jit(solution)/shard_map/while/body/eval_jaxpr/kmn,kcn->kmc/dot_general | solution.py:44
  90.4 1.1 fusion.109
  91.6 18.3 %while.42 = (s32[]{:T(128)}, f32[3,1,64,64]{2,3,1,0:T(8,128)S(1)}, bf16[1024,2048]{1,0:T(8,128)(2,1)}, bf16[3,1,64,64]{3,2,1,0:T(8,128)(2,1)S(1)}, bf16[1,64,204...) while((s32[]{:T(128)}, f32[3,1,64,64]{2,3,1,0:T(8,128)S(1)}, ...), condition=%wide.region_5.6_spmd, body=%wide.region_4.5_spmd.sunk | while | flops 568524800 | bytes 5947493 | solution.py:49
  91.6 0.2 convolution_convert_fusion.10
  91.8 4.7 %fusion.117 = bf16[1024,64]{1,0:T(8,128)(2,1)S(1)} fusion(bf16[1024,2048]{1,0:T(8,128)(2,1)} %get-tuple-element.488, bf16[64,2048]{1,0:T(8,128)(2,1)S(1)} %convolution_convert_fusion.10, bf16[1,64,2048]{2,1,0:T(8,128)(2,1)} %get-tuple-element.492, bf16[1,64,1024]{2,1,0:T(8,128)(2,1)S(1)} %get-tuple-element.491), kind=kOutput, calls=%fused_computation.32.clone.1 | convolution fusion | flops 543227904 | bytes 4980736 | tf_op jit(solution)/shard_map/while/body/eval_jaxpr/kmn,kcn->kmc/dot_general | solution.py:44
  96.5 1.1 fusion.118
  97.7 0.2 convolution_convert_fusion.10
  97.9 4.7 %fusion.117 = bf16[1024,64]{1,0:T(8,128)(2,1)S(1)} fusion(bf16[1024,2048]{1,0:T(8,128)(2,1)} %get-tuple-element.488, bf16[64,2048]{1,0:T(8,128)(2,1)S(1)} %convolution_convert_fusion.10, bf16[1,64,2048]{2,1,0:T(8,128)(2,1)} %get-tuple-element.492, bf16[1,64,1024]{2,1,0:T(8,128)(2,1)S(1)} %get-tuple-element.491), kind=kOutput, calls=%fused_computation.32.clone.1 | convolution fusion | flops 543227904 | bytes 4980736 | tf_op jit(solution)/shard_map/while/body/eval_jaxpr/kmn,kcn->kmc/dot_general | solution.py:44
  102.6 1.1 fusion.118
  103.8 0.2 convolution_convert_fusion.10
  104.0 4.7 %fusion.117 = bf16[1024,64]{1,0:T(8,128)(2,1)S(1)} fusion(bf16[1024,2048]{1,0:T(8,128)(2,1)} %get-tuple-element.488, bf16[64,2048]{1,0:T(8,128)(2,1)S(1)} %convolution_convert_fusion.10, bf16[1,64,2048]{2,1,0:T(8,128)(2,1)} %get-tuple-element.492, bf16[1,64,1024]{2,1,0:T(8,128)(2,1)S(1)} %get-tuple-element.491), kind=kOutput, calls=%fused_computation.32.clone.1 | convolution fusion | flops 543227904 | bytes 4980736 | tf_op jit(solution)/shard_map/while/body/eval_jaxpr/kmn,kcn->kmc/dot_general | solution.py:44
  108.7 1.1 fusion.118
  109.9 18.3 %while.43 = (s32[]{:T(128)}, f32[3,1,64,64]{2,3,1,0:T(8,128)S(1)}, bf16[1024,2048]{1,0:T(8,128)(2,1)}, bf16[3,1,64,64]{3,2,1,0:T(8,128)(2,1)S(1)}, bf16[1,64,204...) while((s32[]{:T(128)}, f32[3,1,64,64]{2,3,1,0:T(8,128)S(1)}, ...), condition=%wide.region_7.8_spmd, body=%wide.region_6.7_spmd.sunk | while | flops 568524800 | bytes 5947493 | solution.py:49
  109.9 0.2 convolution_convert_fusion.11
  110.1 4.7 %fusion.126 = bf16[1024,64]{1,0:T(8,128)(2,1)S(1)} fusion(bf16[1024,2048]{1,0:T(8,128)(2,1)} %get-tuple-element.461, bf16[64,2048]{1,0:T(8,128)(2,1)S(1)} %convolution_convert_fusion.11, bf16[1,64,2048]{2,1,0:T(8,128)(2,1)} %get-tuple-element.465, bf16[1,64,1024]{2,1,0:T(8,128)(2,1)S(1)} %get-tuple-element.464), kind=kOutput, calls=%fused_computation.46.clone.1 | convolution fusion | flops 543227904 | bytes 4980736 | tf_op jit(solution)/shard_map/while/body/eval_jaxpr/kmn,kcn->kmc/dot_general | solution.py:44
  114.9 1.1 fusion.127
  116.0 0.2 convolution_convert_fusion.11
  116.2 4.7 %fusion.126 = bf16[1024,64]{1,0:T(8,128)(2,1)S(1)} fusion(bf16[1024,2048]{1,0:T(8,128)(2,1)} %get-tuple-element.461, bf16[64,2048]{1,0:T(8,128)(2,1)S(1)} %convolution_convert_fusion.11, bf16[1,64,2048]{2,1,0:T(8,128)(2,1)} %get-tuple-element.465, bf16[1,64,1024]{2,1,0:T(8,128)(2,1)S(1)} %get-tuple-element.464), kind=kOutput, calls=%fused_computation.46.clone.1 | convolution fusion | flops 543227904 | bytes 4980736 | tf_op jit(solution)/shard_map/while/body/eval_jaxpr/kmn,kcn->kmc/dot_general | solution.py:44
  120.9 1.1 fusion.127
  122.1 0.2 convolution_convert_fusion.11
  122.3 4.7 %fusion.126 = bf16[1024,64]{1,0:T(8,128)(2,1)S(1)} fusion(bf16[1024,2048]{1,0:T(8,128)(2,1)} %get-tuple-element.461, bf16[64,2048]{1,0:T(8,128)(2,1)S(1)} %convolution_convert_fusion.11, bf16[1,64,2048]{2,1,0:T(8,128)(2,1)} %get-tuple-element.465, bf16[1,64,1024]{2,1,0:T(8,128)(2,1)S(1)} %get-tuple-element.464), kind=kOutput, calls=%fused_computation.46.clone.1 | convolution fusion | flops 543227904 | bytes 4980736 | tf_op jit(solution)/shard_map/while/body/eval_jaxpr/kmn,kcn->kmc/dot_general | solution.py:44
  127.0 1.1 fusion.127
  128.3 0.1 reshape.279
  128.4 5.9 %copy.7 = f32[3,1,4096]{1,0,2:T(4,128)} copy(f32[3,1,4096]{2,1,0:T(1,128)S(1)} %reshape.279) | data formatting | bytes 98304
  134.3 9.8 %bitcast_reduce_fusion = f32[4096,3]{1,0:T(8,128)} fusion(f32[3,1,4096]{1,0,2:T(4,128)} %copy.7), kind=kLoop, calls=%fused_computation.56 | loop fusion | bytes 98304
  144.2 28.3 %reduce-scatter.4.cloned.1.call-done = f32[2048,3]{1,0:T(8,128)} async-done(((f32[4096,3]{1,0:T(8,128)}), f32[2048,3]{1,0:T(8,128)}) %reduce-scatter.4.cloned.1.call-update) | async-done | bytes 24592
  172.5 5.1 %reshape_bitcast_fusion = f32[3,1,2048]{1,0,2:T(4,128)} fusion(f32[2048,3]{1,0:T(8,128)} %reduce-scatter.4.cloned.1.call-done), kind=kLoop, calls=%fused_computation.57 | loop fusion | bytes 49152
  177.6 4.2 %copy.8 = f32[3,1,2048]{2,1,0:T(1,128)} copy(f32[3,1,2048]{1,0,2:T(4,128)} %reshape_bitcast_fusion) | data formatting | bytes 49152
  (26 shorter events, 0.3 us)
Async XLA Ops:
  6.5 166.0 %reduce-scatter.4.cloned.1.call-start = ((), (), s32[]{:S(2)}) async-start(), calls=%async_computation.1 | async-start | bytes 3145728
  12.7 16.7 %collective-permute-start = (bf16[3,1,4096]{2,1,0:T(2,128)(2,1)S(1)}, bf16[3,1,4096]{2,1,0:T(2,128)(2,1)S(1)}, u32[]{:S(2)}, u32[]{:S(2)}) collective-permute-start(bf16[3,1,4096]{2,1,0:T(2,128)(2,1)S(1)} %all_gather.6), channel_id=1, source_target_pairs={{0,2},{2,4},{4,6},{6,8},{8,10},{10,12},{12,14},{14,16},{16,18},{18... | collective-permute-start | bytes 73736 | tf_op jit(solution)/shard_map/ppermute | solution.py:12
  12.8 29.3 %collective-permute-start.3 = (bf16[3,1,4096]{2,1,0:T(2,128)(2,1)S(1)}, bf16[3,1,4096]{2,1,0:T(2,128)(2,1)S(1)}, u32[]{:S(2)}, u32[]{:S(2)}) collective-permute-start(bf16[3,1,4096]{2,1,0:T(2,128)(2,1)S(1)} %all_gather.6), channel_id=1, source_target_pairs={{0,30},{2,0},{4,2},{6,4},{8,6},{10,8},{12,10},{14,12},{16,14},{18,... | collective-permute-start | bytes 73736 | tf_op jit(solution)/shard_map/ppermute | solution.py:12
  17.2 29.6 %collective-permute-start.6 = (bf16[3,1,4096]{2,1,0:T(2,128)(2,1)S(1)}, bf16[3,1,4096]{2,1,0:T(2,128)(2,1)S(1)}, u32[]{:S(2)}, u32[]{:S(2)}) collective-permute-start(bf16[3,1,4096]{2,1,0:T(2,128)(2,1)S(1)} %all_gather.6), channel_id=1, source_target_pairs={{0,4},{2,6},{4,8},{6,10},{8,12},{10,14},{12,16},{14,18},{16,20},{1... | collective-permute-start | bytes 73736 | tf_op jit(solution)/shard_map/ppermute | solution.py:12
  17.2 30.4 %collective-permute-start.9 = (bf16[3,1,4096]{2,1,0:T(2,128)(2,1)S(1)}, bf16[3,1,4096]{2,1,0:T(2,128)(2,1)S(1)}, u32[]{:S(2)}, u32[]{:S(2)}) collective-permute-start(bf16[3,1,4096]{2,1,0:T(2,128)(2,1)S(1)} %all_gather.6), channel_id=1, source_target_pairs={{0,28},{2,30},{4,0},{6,2},{8,4},{10,6},{12,8},{14,10},{16,12},{18,... | collective-permute-start | bytes 73736 | tf_op jit(solution)/shard_map/ppermute | solution.py:12
  29.4 18.6 %collective-permute-start.1 = (bf16[1,64,2048]{2,1,0:T(8,128)(2,1)}, bf16[1,64,2048]{2,1,0:T(8,128)(2,1)S(1)}, u32[]{:S(2)}, u32[]{:S(2)}) collective-permute-start(bf16[1,64,2048]{2,1,0:T(8,128)(2,1)} %all_gather.7), channel_id=1, source_target_pairs={{0,2},{2,4},{4,6},{6,8},{8,10},{10,12},{12,14},{14,16},{16,18},{18... | collective-permute-start | bytes 786440 | tf_op jit(solution)/shard_map/ppermute | solution.py:12
  29.4 18.5 %collective-permute-start.2 = (bf16[1,64,1024]{2,1,0:T(8,128)(2,1)}, bf16[1,64,1024]{2,1,0:T(8,128)(2,1)S(1)}, u32[]{:S(2)}, u32[]{:S(2)}) collective-permute-start(bf16[1,64,1024]{2,1,0:T(8,128)(2,1)} %param.14), channel_id=1, source_target_pairs={{0,2},{2,4},{4,6},{6,8},{8,10},{10,12},{12,14},{14,16},{16,18},{18... | collective-permute-start | bytes 393224 | tf_op jit(solution)/shard_map/ppermute | solution.py:12
  42.1 31.2 %collective-permute-start.4 = (bf16[1,64,2048]{2,1,0:T(8,128)(2,1)}, bf16[1,64,2048]{2,1,0:T(8,128)(2,1)S(1)}, u32[]{:S(2)}, u32[]{:S(2)}) collective-permute-start(bf16[1,64,2048]{2,1,0:T(8,128)(2,1)} %all_gather.7), channel_id=1, source_target_pairs={{0,30},{2,0},{4,2},{6,4},{8,6},{10,8},{12,10},{14,12},{16,14},{18,... | collective-permute-start | bytes 786440 | tf_op jit(solution)/shard_map/ppermute | solution.py:12
  46.8 24.2 %collective-permute-start.5 = (bf16[1,64,1024]{2,1,0:T(8,128)(2,1)}, bf16[1,64,1024]{2,1,0:T(8,128)(2,1)S(1)}, u32[]{:S(2)}, u32[]{:S(2)}) collective-permute-start(bf16[1,64,1024]{2,1,0:T(8,128)(2,1)} %param.14), channel_id=1, source_target_pairs={{0,30},{2,0},{4,2},{6,4},{8,6},{10,8},{12,10},{14,12},{16,14},{18,... | collective-permute-start | bytes 393224 | tf_op jit(solution)/shard_map/ppermute | solution.py:12
  47.6 43.9 %collective-permute-start.7 = (bf16[1,64,2048]{2,1,0:T(8,128)(2,1)}, bf16[1,64,2048]{2,1,0:T(8,128)(2,1)S(1)}, u32[]{:S(2)}, u32[]{:S(2)}) collective-permute-start(bf16[1,64,2048]{2,1,0:T(8,128)(2,1)} %all_gather.7), channel_id=1, source_target_pairs={{0,4},{2,6},{4,8},{6,10},{8,12},{10,14},{12,16},{14,18},{16,20},{1... | collective-permute-start | bytes 786440 | tf_op jit(solution)/shard_map/ppermute | solution.py:12
  48.0 43.6 %collective-permute-start.8 = (bf16[1,64,1024]{2,1,0:T(8,128)(2,1)}, bf16[1,64,1024]{2,1,0:T(8,128)(2,1)S(1)}, u32[]{:S(2)}, u32[]{:S(2)}) collective-permute-start(bf16[1,64,1024]{2,1,0:T(8,128)(2,1)} %param.14), channel_id=1, source_target_pairs={{0,4},{2,6},{4,8},{6,10},{8,12},{10,14},{12,16},{14,18},{16,20},{1... | collective-permute-start | bytes 393224 | tf_op jit(solution)/shard_map/ppermute | solution.py:12
  48.1 61.8 %collective-permute-start.10 = (bf16[1,64,2048]{2,1,0:T(8,128)(2,1)}, bf16[1,64,2048]{2,1,0:T(8,128)(2,1)S(1)}, u32[]{:S(2)}, u32[]{:S(2)}) collective-permute-start(bf16[1,64,2048]{2,1,0:T(8,128)(2,1)} %all_gather.7), channel_id=1, source_target_pairs={{0,28},{2,30},{4,0},{6,2},{8,4},{10,6},{12,8},{14,10},{16,12},{18,... | collective-permute-start | bytes 786440 | tf_op jit(solution)/shard_map/ppermute | solution.py:12
  71.1 38.8 %collective-permute-start.11 = (bf16[1,64,1024]{2,1,0:T(8,128)(2,1)}, bf16[1,64,1024]{2,1,0:T(8,128)(2,1)S(1)}, u32[]{:S(2)}, u32[]{:S(2)}) collective-permute-start(bf16[1,64,1024]{2,1,0:T(8,128)(2,1)} %param.14), channel_id=1, source_target_pairs={{0,28},{2,30},{4,0},{6,2},{8,4},{10,6},{12,8},{14,10},{16,12},{18,... | collective-permute-start | bytes 393224 | tf_op jit(solution)/shard_map/ppermute | solution.py:12
Sparse Core Ops, SparseCore 0:
  144.3 28.1 reduce-scatter.3
where the time goes:
time: 189 us
  matrix products  72.6 us (38%)
  local copies, waits for them, and re-layouts  38.1 us (20%)
  waiting for transfers between devices  28.4 us (15%)
  starting transfers between devices  21.3 us (11%)
  between operations  13.6 us (7%)
  blocking collectives  13 us (7%)
    dot_general x12, matrix products, per_vector(): jnp.einsum('kmn,kcn->kmc', weighted, con_home, preferred_element_type=jnp...  56.5 us
    unnamed x2, waiting for transfers between devices  28.3 us
    unnamed x4, local copies, waits for them, and re-layouts  25.1 us
    ppermute x12, starting transfers between devices, passed_along(): return lax.ppermute(value, axis, pairs)  21.3 us
    dot_general x12, matrix products, per_vector(): jnp.einsum('kvm,kmc->kvc', phi_val, folded, preferred_element_type=jnp.fl...  13.7 us
    squeeze x1, local copies, waits for them, and re-layouts, local(): kernel = screened[offset]  12.4 us
    all_gather x1, blocking collectives, local(): lax.all_gather(phi_con, 'mu', axis=2, tiled=True)  7.5 us
    all_gather x1, blocking collectives, local(): lax.all_gather(vec_coded, 'mu', axis=2, tiled=True)  5.45 us
  transfers between devices with their start and end apart: 13, of which 1 were waited for; matrix products, arithmetic and copies ran while one was open for 36% of the time, Pallas kernels for 0%

commit v1 on v0

v1 whole, which is shorter than its diff:
```python
import functools

import jax
import jax.numpy as jnp
from jax import lax
from jax.experimental import pallas as pl
from jax.experimental.pallas import tpu as pltpu
from jax.sharding import PartitionSpec as P

BF16, F32 = jnp.bfloat16, jnp.float32
VMEM_SPEC = pl.BlockSpec(memory_space=pltpu.VMEM)
SMEM_SPEC = pl.BlockSpec(memory_space=pltpu.SMEM)
HBM_SPEC = pl.BlockSpec(memory_space=pl.ANY)
MIB = 1 << 20
NEAR, FAR, AHEAD, BEHIND = range(4)


def contract(left, right, left_dim, right_dim):
    dims = (((left_dim,), (right_dim,)), ((), ()))
    return lax.dot_general(left, right, dims, preferred_element_type=F32)


def screened_copy(screened, info, slot, part, cols, buffer, sem):
    count = screened.shape[2] // cols
    home = lax.rem(info[0] + part, count)
    columns = pl.ds(pl.multiple_of(home * cols, cols), cols)
    return pltpu.make_async_copy(
        screened.at[info[1 + slot], :, columns], buffer.at[:, pl.ds(part * cols, cols)], sem
    )


def first_kernel(count, info, *refs):
    vec_parts, con_parts = refs[:count], refs[count : 2 * count]
    val_home, val_near, screened, pairs, folded, vec_all, buffer, sems = refs[2 * count :]
    vec_count, rows, conduction = vec_parts[0].shape
    cols = con_parts[0].shape[1]
    for part in range(count):
        screened_copy(screened, info, NEAR, part, cols, buffer, sems.at[part]).start()
    for part in range(count):
        offset = pl.multiple_of(lax.rem(info[0] + part, count) * rows, rows)
        for s in range(vec_count):
            vec_all[s, pl.ds(offset, rows), :] = vec_parts[part][s].astype(F32)
    for s in range(vec_count):
        half = contract(val_home[...], vec_all[s].astype(BF16), 0, 0).astype(BF16)
        for part in range(count):
            pairs[s, :, pl.ds(part * cols, cols)] = contract(
                half, con_parts[part][...], 1, 0
            ).astype(BF16)
    for part in range(count):
        screened_copy(screened, info, NEAR, part, cols, buffer, sems.at[part]).wait()
    valence = val_near.shape[0]
    for s in range(vec_count):
        folded[pl.ds(s * valence, valence), :] = contract(
            val_near[...], buffer[...] * pairs[s], 1, 0
        ).astype(BF16)


def fold_kernel(count, slots, info, *refs):
    used = len(slots)
    pairs, screened = refs[:2]
    vals, foldeds = refs[2 : 2 + used], refs[3 + used : 3 + 2 * used]
    buffers, sems = refs[-2:]
    vec_count, _, points = pairs.shape
    cols = points // count
    valence = vals[0].shape[0]
    for i, slot in enumerate(slots):
        for part in range(count):
            screened_copy(screened, info, slot, part, cols, buffers.at[i], sems.at[i, part]).start()
    for i, slot in enumerate(slots):
        for part in range(count):
            screened_copy(screened, info, slot, part, cols, buffers.at[i], sems.at[i, part]).wait()
        for s in range(vec_count):
            foldeds[i][pl.ds(s * valence, valence), :] = contract(
                vals[i][...], buffers[i] * pairs[s], 1, 0
            ).astype(BF16)


def result_kernel(count, used, info, *refs):
    foldeds, cons = refs[:used], refs[used : used + used * count]
    outs, work = refs[used + used * count : -1], refs[-1]
    vec_count, rows, _ = outs[0].shape
    valence = foldeds[0].shape[0] // vec_count
    cols = cons[0].shape[1]
    for i in range(used):
        total = contract(foldeds[i][:, pl.ds(0, cols)], cons[i * count][...], 1, 1)
        for part in range(1, count):
            total += contract(
                foldeds[i][:, pl.ds(part * cols, cols)], cons[i * count + part][...], 1, 1
            )
        work[i] = total
        for part in range(count):
            offset = lax.rem(info[0] + part, count) * rows
            for s in range(vec_count):
                start = pl.multiple_of(s * valence + offset, 8)
                outs[i * count + part][s] = work[i, pl.ds(start, rows), :]


def moved(value, pairs_of):
    ka, mu = lax.axis_size("ka"), lax.axis_size("mu")
    pairs = []
    for k in range(ka):
        for m in range(mu):
            k_to, m_to = pairs_of(k, m)
            pairs.append((k * mu + m, (k_to % ka) * mu + m_to % mu))
    return lax.ppermute(value, ("ka", "mu"), pairs)


def target_of(slot, k):
    sign = 1 - 2 * (k % 2)
    return k + sign * {NEAR: 1, FAR: -1, AHEAD: 2, BEHIND: -2}[slot]


def local(vectors, phi_val, phi_con, screened, partner):
    del partner
    ka, count = lax.axis_size("ka"), lax.axis_size("mu")
    vec_count, local_k, local_pairs = vectors.shape
    _, valence, rows_m = phi_val.shape
    _, conduction, cols = phi_con.shape
    points = screened.shape[2]
    if local_k != 1 or ka % 2:
        raise ValueError("unsupported shapes")
    rows = local_pairs // conduction

    me, parity = lax.axis_index("mu"), lax.axis_index("ka") % 2
    info = jnp.concatenate([me[None], jnp.arange(4) ^ parity]).astype(jnp.int32)

    def from_slot(slot):
        back = {NEAR: NEAR, FAR: FAR, AHEAD: BEHIND, BEHIND: AHEAD}[slot]
        if slot in (AHEAD, BEHIND):
            return lambda k, m: (target_of(back, k), m)
        return lambda k, m: (target_of(slot, k), m)

    def over_mu(value):
        return [value] + [
            moved(value, lambda k, m, t=t: (k, m - t)) for t in range(1, count)
        ]

    val_home, con_home = phi_val[0], phi_con[0]
    vec_home = vectors.astype(BF16).reshape(vec_count, rows, conduction)
    vec_parts = over_mu(vec_home)
    con_parts = over_mu(con_home)
    val = {s: moved(val_home, from_slot(s)) for s in (NEAR, AHEAD, BEHIND)}
    con = {s: moved(con_home, from_slot(s)) for s in (AHEAD, BEHIND)}
    val[FAR] = moved(val[AHEAD], from_slot(NEAR))
    con_all = {s: over_mu(con[s]) for s in (AHEAD, BEHIND)}
    con_all[NEAR] = [moved(part, from_slot(NEAR)) for part in con_parts]
    con_all[FAR] = [moved(part, from_slot(NEAR)) for part in con_all[AHEAD]]

    pairs_type = jax.ShapeDtypeStruct((vec_count, rows_m, points), BF16)
    folded_type = jax.ShapeDtypeStruct((vec_count * valence, points), BF16)
    result_type = jax.ShapeDtypeStruct((vec_count, rows, conduction), F32)
    fold_flops = 2 * vec_count * valence * rows_m * points

    def params(mib):
        return pltpu.CompilerParams(vmem_limit_bytes=mib * MIB)

    pairs, folded_near = pl.pallas_call(
        functools.partial(first_kernel, count),
        out_shape=[pairs_type, folded_type],
        in_specs=[SMEM_SPEC] + [VMEM_SPEC] * (2 * count + 2) + [HBM_SPEC],
        out_specs=[VMEM_SPEC] * 2,
        scratch_shapes=[
            pltpu.VMEM((vec_count, valence, conduction), F32),
            pltpu.VMEM((rows_m, points), BF16),
            pltpu.SemaphoreType.DMA((count,)),
        ],
        compiler_params=params(30),
        cost_estimate=pl.CostEstimate(flops=8 * fold_flops, bytes_accessed=4 * MIB, transcendentals=0),
        name="first",
    )(info, *vec_parts, *con_parts, val_home, val[NEAR], screened)

    def fold(pairs, *slots):
        used = len(slots)
        out = pl.pallas_call(
            functools.partial(fold_kernel, count, slots),
            out_shape=[pairs_type] + [folded_type] * used,
            in_specs=[SMEM_SPEC, VMEM_SPEC, HBM_SPEC] + [VMEM_SPEC] * used,
            out_specs=[VMEM_SPEC] * (1 + used),
            scratch_shapes=[
                pltpu.VMEM((used, rows_m, points), BF16),
                pltpu.SemaphoreType.DMA((used, count)),
            ],
            input_output_aliases={1: 0},
            compiler_params=params(30),
            cost_estimate=pl.CostEstimate(
                flops=4 * used * fold_flops, bytes_accessed=4 * used * MIB, transcendentals=0
            ),
            name="fold%d" % used,
        )(info, pairs, screened, *[val[s] for s in slots])
        return out[0], out[1:]

    def results(foldeds, *slots):
        used = len(slots)
        out = pl.pallas_call(
            functools.partial(result_kernel, count, used),
            out_shape=[result_type] * (used * count),
            in_specs=[SMEM_SPEC] + [VMEM_SPEC] * (used + used * count),
            out_specs=[VMEM_SPEC] * (used * count),
            scratch_shapes=[pltpu.VMEM((used, vec_count * valence, conduction), F32)],
            compiler_params=params(10),
            cost_estimate=pl.CostEstimate(
                flops=2 * used * fold_flops // 8, bytes_accessed=MIB, transcendentals=0
            ),
            name="result%d" % used,
        )(info, *foldeds, *[part for s in slots for part in con_all[s]])
        received = []
        for i, slot in enumerate(slots):
            for part in range(count):
                received.append(
                    moved(
                        out[i * count + part],
                        lambda k, m, slot=slot, part=part: (target_of(slot, k), m + part),
                    )
                )
        return received

    pairs, (folded_ahead, folded_behind) = fold(pairs, AHEAD, BEHIND)
    received = results((folded_near, folded_ahead, folded_behind), NEAR, AHEAD, BEHIND)
    pairs, (folded_far,) = fold(pairs, FAR)
    received += results((folded_far,), FAR)
    total = functools.reduce(jnp.add, received)
    return total.reshape(vec_count, 1, local_pairs)


def solution(mesh):
    placed = (
        P(None, "ka", "mu"),
        P("ka", None, "mu"),
        P("ka", None, "mu"),
        P(None, "mu", None),
        P("ka", None),
    )
    return jax.shard_map(
        local, mesh=mesh, in_specs=placed, out_specs=P(None, "ka", "mu"), check_vma=False
    )
```

time: 189 us -> 66.5 us (0.35)
  matrix products: 72.6 us -> 0 us
  local copies, waits for them, and re-layouts: 38.1 us -> 2.6 us
  Pallas kernels: 0 us -> 24.4 us
  waiting for transfers between devices: 28.4 us -> 5.99 us
  between operations: 13.6 us -> 0.13 us
  blocking collectives: 13 us -> 0 us
  starting transfers between devices: 21.3 us -> 32.2 us
    dot_general x36 -> x0, matrix products: 72.6 us -> none  [the longest x12 56.5 us: per_vector(): jnp.einsum('kmn,kcn->kmc', weighted, con_home, preferred_element_type=jnp...]
    unnamed x2 -> x0, waiting for transfers between devices: 28.3 us -> none
    pallas_call x0 -> x5, Pallas kernels: none -> 24.4 us  [the longest x2 13.4 us: fold(): pl.pallas_call(functools.partial(fold_kernel, count, slots), out_shape=[p...]
    unnamed x4, local copies, waits for them, and re-layouts: 25.1 us -> 1.8 us
    all_gather x2 -> x0, blocking collectives: 13 us -> none  [the longest x1 7.5 us: local(): lax.all_gather(phi_con, 'mu', axis=2, tiled=True)]
    squeeze x1 -> x0, local copies, waits for them, and re-layouts: 12.4 us -> none  [local(): kernel = screened[offset]]
    ppermute x12 -> x22, starting transfers between devices: 21.3 us -> 32.2 us  [moved(): return lax.ppermute(value, ('ka', 'mu'), pairs)]
    ppermute x12 -> x22, waiting for transfers between devices: 0.03 us -> 5.99 us  [moved(): return lax.ppermute(value, ('ka', 'mu'), pairs)]
  transfers between devices with their start and end apart: 13 -> 22, of which waited for: 1 -> 3; matrix products, arithmetic and copies ran while one was open for 36% -> 1% of each run, Pallas kernels for 0% -> 37%
where the time goes in v1:
time: 66.5 us; the launch traced here: 66.3 us
  starting transfers between devices  32.2 us (48%)
  Pallas kernels  24.4 us (37%)
  waiting for transfers between devices  5.99 us (9%)
  local copies, waits for them, and re-layouts  2.6 us (4%)
  other arithmetic  0.92 us (1%)
    ppermute x22, starting transfers between devices, moved(): return lax.ppermute(value, ('ka', 'mu'), pairs)  32.2 us
    pallas_call x2, Pallas kernels, fold(): pl.pallas_call(functools.partial(fold_kernel, count, slots), out_shape=[p...  13.4 us
    pallas_call x1, Pallas kernels, local(): pl.pallas_call(functools.partial(first_kernel, count), out_shape=[pairs_t...  8.72 us
    ppermute x22, waiting for transfers between devices, moved(): return lax.ppermute(value, ('ka', 'mu'), pairs)  5.99 us
    pallas_call x2, Pallas kernels, results(): pl.pallas_call(functools.partial(result_kernel, count, used), out_shape=[...  2.24 us
    unnamed x4, local copies, waits for them, and re-layouts  1.8 us
  transfers between devices with their start and end apart: 22, of which 3 were waited for; matrix products, arithmetic and copies ran while one was open for 1% of the time, Pallas kernels for 37%

profile of v1, /device:TPU:0, one launch (start us, length us, event | category | flops | bytes accessed | tf_op | source)
XLA Modules:
  0.0 66.3 jit_solution(15012426356238618470)
XLA Ops:
  0.0 0.5 collective-permute-start.2
  0.5 5.5 %collective-permute-start.3 = (bf16[64,1024]{1,0:T(8,128)(2,1)}, bf16[64,1024]{1,0:T(8,128)(2,1)S(1)}, u32[]{:S(2)}, u32[]{:S(2)}) collective-permute-start(bf16[64,1024]{1,0:T(8,128)(2,1)} %bitcast.4), channel_id=1, source_target_pairs={{0,28},{1,29},{2,6},{3,7},{4,0},{5,1},{6,10},{7,11},{8,4},{9,5},{1... | collective-permute-start | bytes 393224 | tf_op jit(solution)/shard_map/ppermute | solution.py:105
  6.0 0.0 collective-permute-start.4
  6.0 1.5 %collective-permute-start.1 = (bf16[64,1024]{1,0:T(8,128)(2,1)}, bf16[64,1024]{1,0:T(8,128)(2,1)S(1)}, u32[]{:S(2)}, u32[]{:S(2)}) collective-permute-start(bf16[64,1024]{1,0:T(8,128)(2,1)} %bitcast.7), channel_id=1, source_target_pairs={{0,1},{1,0},{2,3},{3,2},{4,5},{5,4},{6,7},{7,6},{8,9},{9,8},{10,11... | collective-permute-start | bytes 393224 | tf_op jit(solution)/shard_map/ppermute | solution.py:105
  7.5 0.8 %convert_reduce_fusion = bf16[3,2048]{1,0:T(4,128)(2,1)S(1)} fusion(f32[3,1,2048]{2,1,0:T(1,128)} %param.5), kind=kLoop, calls=%fused_computation.1 | loop fusion | flops 6144 | bytes 36864 | tf_op jit(solution)/shard_map/convert_element_type | solution.py:139
  8.3 0.1 reshape.6.refs_0_
  8.4 0.6 collective-permute-start
  9.0 0.1 pad_add_fusion.info
  9.1 3.3 %collective-permute-done.refs_1_ = bf16[3,32,64]{2,1,0:T(8,128)(2,1)S(1)} collective-permute-done((bf16[3,32,64]{2,1,0:T(8,128)(2,1)S(1)}, bf16[3,32,64]{2,1,0:T(8,128)(2,1)S(1)}, u32[]{:S(2)}, u32[]{:S(2)}) %collective-permute-start) | collective-permute-done | bytes 12320 | tf_op jit(solution)/shard_map/ppermute | solution.py:105
  12.4 4.7 %collective-permute-start.7 = (bf16[64,1024]{1,0:T(8,128)(2,1)}, bf16[64,1024]{1,0:T(8,128)(2,1)S(1)}, u32[]{:S(2)}, u32[]{:S(2)}) collective-permute-start(bf16[64,1024]{1,0:T(8,128)(2,1)} %bitcast.8), channel_id=1, source_target_pairs={{0,28},{1,29},{2,6},{3,7},{4,0},{5,1},{6,10},{7,11},{8,4},{9,5},{1... | collective-permute-start | bytes 393224 | tf_op jit(solution)/shard_map/ppermute | solution.py:105
  17.0 0.0 collective-permute-done.1.refs_3_
  17.0 0.0 collective-permute-start.9
  17.0 0.0 collective-permute-done.2.refs_5_
  17.1 0.1 collective-permute-start.5
  17.1 0.0 copy-start
  17.1 0.9 %copy-done = bf16[1,64,1024]{2,1,0:T(8,128)(2,1)S(1)} copy-done((bf16[1,64,1024]{2,1,0:T(8,128)(2,1)S(1)}, bf16[1,64,1024]{2,1,0:T(8,128)(2,1)}, u32[]{:S(2)}) %copy-start) | copy-done | bytes 131096
  18.0 0.0 copy-start.1
  18.0 0.9 %copy-done.1 = bf16[1,64,1024]{2,1,0:T(8,128)(2,1)S(1)} copy-done((bf16[1,64,1024]{2,1,0:T(8,128)(2,1)S(1)}, bf16[1,64,1024]{2,1,0:T(8,128)(2,1)}, u32[]{:S(2)}) %copy-start.1) | copy-done | bytes 131096
  18.9 8.7 %first.1 = (bf16[3,1024,2048]{2,1,0:T(8,128)(2,1)S(1)}, bf16[192,2048]{1,0:T(8,128)(2,1)S(1)}) custom-call(s32[5]{0:T(128)S(1)} %pad_add_fusion.info, bf16[3,32,64]{2,1,0:T(8,128)(2,1)S(1)} %reshape.6.refs_0_, bf16[3,32,64]{2,1,0:T(8,128)(2,1)S(1)} %collective-permute-done.refs_1_, bf16[64,1024]{1,0:T(8,128)(2,1)S(1)} %bitcast.11, ...), custom_call_target="tpu_custom_call" | custom-call | flops 6442450944 | bytes 4194304 | tf_op jit(solution)/shard_map/first/pallas_call | solution.py:157
  27.7 0.0 collective-permute-done.3.refs_2_
  27.7 0.6 collective-permute-start.6
  28.2 0.0 collective-permute-done.7.refs_5_
  28.2 0.7 collective-permute-start.8
  28.9 0.0 collective-permute-done.9.refs_7_
  28.9 1.4 %collective-permute-start.10 = (bf16[64,1024]{1,0:T(8,128)(2,1)S(1)}, bf16[64,1024]{1,0:T(8,128)(2,1)S(1)}, u32[]{:S(2)}, u32[]{:S(2)}) collective-permute-start(bf16[64,1024]{1,0:T(8,128)(2,1)S(1)} %collective-permute-done.9.refs_7_), channel_id=1, source_target_pairs={{0,1},{1,0},{2,3},{3,2},{4,5},{5,4},{6,7},{7,6},{8,9},{9,8},{10,11... | collective-permute-start | bytes 393224 | tf_op jit(solution)/shard_map/ppermute | solution.py:105
  30.3 0.0 collective-permute-done.4.refs_3_
  30.3 0.0 collective-permute-start.17
  30.3 8.1 %fold2.1 = (bf16[3,1024,2048]{2,1,0:T(8,128)(2,1)S(1)}, bf16[192,2048]{1,0:T(8,128)(2,1)S(1)}, bf16[192,2048]{1,0:T(8,128)(2,1)S(1)}) custom-call(s32[5]{0:T(128)S(1)} %pad_add_fusion.info, bf16[3,1024,2048]{2,1,0:T(8,128)(2,1)S(1)} %get-tuple-element.20.refs_0_, bf16[4,1024,2048]{2,1,0:T(8,128)(2,1)} %refs_1_.3, ...), custom_call_target="tpu_custom_call", output_to_operand_aliasing={{0}: (1, {})} | custom-call | flops 6442450944 | bytes 8388608 | tf_op jit(solution)/shard_map/fold2/pallas_call | solution.py:174
  38.3 0.0 collective-permute-done.5.refs_3_
  38.4 0.6 collective-permute-start.18
  38.9 0.0 collective-permute-done.8.refs_6_
  38.9 0.0 collective-permute-done.10.refs_8_
  38.9 0.0 collective-permute-done.6.refs_4_
  38.9 1.3 %result3.1 = (f32[3,32,64]{2,1,0:T(8,128)S(1)}, f32[3,32,64]{2,1,0:T(8,128)S(1)}, f32[3,32,64]{2,1,0:T(8,128)S(1)}, f32[3,32,64]{2,1,0:T(8,128)S(1)}, f32[3,32,6...) custom-call(s32[5]{0:T(128)S(1)} %pad_add_fusion.info, bf16[192,2048]{1,0:T(8,128)(2,1)S(1)} %get-tuple-element.19.refs_0_, ...), custom_call_target="tpu_custom_call" | custom-call | flops 603979776 | bytes 1048576 | tf_op jit(solution)/shard_map/result3/pallas_call | solution.py:194
  40.3 0.1 collective-permute-start.11
  40.4 0.7 %collective-permute-start.12 = (f32[3,32,64]{2,1,0:T(8,128)S(1)}, f32[3,32,64]{2,1,0:T(8,128)S(1)}, u32[]{:S(2)}, u32[]{:S(2)}) collective-permute-start(f32[3,32,64]{2,1,0:T(8,128)S(1)} %get-tuple-element.24), channel_id=1, source_target_pairs={{0,3},{1,2},{2,1},{3,0},{4,7},{5,6},{6,5},{7,4},{8,11},{9,10},{10,... | collective-permute-start | bytes 73736 | tf_op jit(solution)/shard_map/ppermute | solution.py:105
  41.1 0.0 collective-permute-start.13
  41.1 0.0 collective-permute-done.17.refs_2_
  41.1 4.4 %collective-permute-start.19 = (bf16[64,1024]{1,0:T(8,128)(2,1)S(1)}, bf16[64,1024]{1,0:T(8,128)(2,1)S(1)}, u32[]{:S(2)}, u32[]{:S(2)}) collective-permute-start(bf16[64,1024]{1,0:T(8,128)(2,1)S(1)} %collective-permute-done.8.refs_6_), channel_id=1, source_target_pairs={{0,2},{1,3},{2,0},{3,1},{4,6},{5,7},{6,4},{7,5},{8,10},{9,11},{10,... | collective-permute-start | bytes 393224 | tf_op jit(solution)/shard_map/ppermute | solution.py:105
  45.6 5.4 %fold1.1 = (bf16[3,1024,2048]{2,1,0:T(8,128)(2,1)S(1)}, bf16[192,2048]{1,0:T(8,128)(2,1)S(1)}) custom-call(s32[5]{0:T(128)S(1)} %pad_add_fusion.info, bf16[3,1024,2048]{2,1,0:T(8,128)(2,1)S(1)} %get-tuple-element.29.refs_0_, bf16[4,1024,2048]{2,1,0:T(8,128)(2,1)} %refs_1_.3, ...), custom_call_target="tpu_custom_call", output_to_operand_aliasing={{0}: (1, {})} | custom-call | flops 3221225472 | bytes 4194304 | tf_op jit(solution)/shard_map/fold1/pallas_call | solution.py:174
  51.0 0.0 collective-permute-done.18.refs_1_
  51.0 0.1 collective-permute-start.14
  51.0 0.0 collective-permute-done.19.refs_2_
  51.1 5.5 %collective-permute-start.15 = (f32[3,32,64]{2,1,0:T(8,128)S(1)}, f32[3,32,64]{2,1,0:T(8,128)S(1)}, u32[]{:S(2)}, u32[]{:S(2)}) collective-permute-start(f32[3,32,64]{2,1,0:T(8,128)S(1)} %get-tuple-element.27), channel_id=1, source_target_pairs={{0,28},{1,29},{2,6},{3,7},{4,0},{5,1},{6,10},{7,11},{8,4},{9,5},{1... | collective-permute-start | bytes 73736 | tf_op jit(solution)/shard_map/ppermute | solution.py:105
  56.6 0.9 %result1.1 = (f32[3,32,64]{2,1,0:T(8,128)S(1)}, f32[3,32,64]{2,1,0:T(8,128)S(1)}) custom-call(s32[5]{0:T(128)S(1)} %pad_add_fusion.info, bf16[192,2048]{1,0:T(8,128)(2,1)S(1)} %get-tuple-element.30.refs_0_, bf16[64,1024]{1,0:T(8,128)(2,1)S(1)} %collective-permute-done.18.refs_1_, bf16[64,1024]{1,0:T(8,128)(2,1)S(1)} %collective-permute-done.19.refs_2_), custom_call_target="tpu_custom_call" | custom-call | flops 201326592 | bytes 1048576 | tf_op jit(solution)/shard_map/result1/pallas_call | solution.py:194
  57.5 0.0 collective-permute-done.11
  57.5 0.1 collective-permute-start.16
  57.6 0.0 collective-permute-done.12
  57.6 0.8 %collective-permute-start.20 = (f32[3,32,64]{2,1,0:T(8,128)S(1)}, f32[3,32,64]{2,1,0:T(8,128)S(1)}, u32[]{:S(2)}, u32[]{:S(2)}) collective-permute-start(f32[3,32,64]{2,1,0:T(8,128)S(1)} %get-tuple-element.31), channel_id=1, source_target_pairs={{0,30},{1,31},{2,4},{3,5},{4,2},{5,3},{6,8},{7,9},{8,6},{9,7},{10,... | collective-permute-start | bytes 73736 | tf_op jit(solution)/shard_map/ppermute | solution.py:105
  58.4 0.0 collective-permute-done.13
  58.4 4.5 %collective-permute-start.21 = (f32[3,32,64]{2,1,0:T(8,128)S(1)}, f32[3,32,64]{2,1,0:T(8,128)S(1)}, u32[]{:S(2)}, u32[]{:S(2)}) collective-permute-start(f32[3,32,64]{2,1,0:T(8,128)S(1)} %get-tuple-element.32), channel_id=1, source_target_pairs={{0,31},{1,30},{2,5},{3,4},{4,3},{5,2},{6,9},{7,8},{8,7},{9,6},{10,... | collective-permute-start | bytes 73736 | tf_op jit(solution)/shard_map/ppermute | solution.py:105
  62.9 0.0 collective-permute-done.14
  62.9 0.0 collective-permute-done.15
  62.9 0.0 collective-permute-done.16
  62.9 1.0 %collective-permute-done.20 = f32[3,32,64]{2,1,0:T(8,128)S(1)} collective-permute-done((f32[3,32,64]{2,1,0:T(8,128)S(1)}, f32[3,32,64]{2,1,0:T(8,128)S(1)}, u32[]{:S(2)}, u32[]{:S(2)}) %collective-permute-start.20) | collective-permute-done | bytes 24608 | tf_op jit(solution)/shard_map/ppermute | solution.py:105
  63.9 1.7 %collective-permute-done.21 = f32[3,32,64]{2,1,0:T(8,128)S(1)} collective-permute-done((f32[3,32,64]{2,1,0:T(8,128)S(1)}, f32[3,32,64]{2,1,0:T(8,128)S(1)}, u32[]{:S(2)}, u32[]{:S(2)}) %collective-permute-start.21) | collective-permute-done | bytes 24608 | tf_op jit(solution)/shard_map/ppermute | solution.py:105
  65.6 0.7 %reshape.8 = f32[3,1,2048]{2,1,0:T(1,128)} reshape(f32[3,32,64]{2,1,0:T(8,128)S(1)} %add_add_fusion) | data formatting | bytes 49152 | tf_op jit(solution)/shard_map/reshape | solution.py:222
  (2 shorter events, 0.0 us)
Async XLA Ops:
  0.0 17.1 %collective-permute-start.2 = (bf16[64,1024]{1,0:T(8,128)(2,1)}, bf16[64,1024]{1,0:T(8,128)(2,1)S(1)}, u32[]{:S(2)}, u32[]{:S(2)}) collective-permute-start(bf16[64,1024]{1,0:T(8,128)(2,1)} %bitcast.3), channel_id=1, source_target_pairs={{0,2},{1,3},{2,0},{3,1},{4,6},{5,7},{6,4},{7,5},{8,10},{9,11},{10,... | collective-permute-start | bytes 393224 | tf_op jit(solution)/shard_map/ppermute | solution.py:105
  0.5 27.2 %collective-permute-start.3 = (bf16[64,1024]{1,0:T(8,128)(2,1)}, bf16[64,1024]{1,0:T(8,128)(2,1)S(1)}, u32[]{:S(2)}, u32[]{:S(2)}) collective-permute-start(bf16[64,1024]{1,0:T(8,128)(2,1)} %bitcast.4), channel_id=1, source_target_pairs={{0,28},{1,29},{2,6},{3,7},{4,0},{5,1},{6,10},{7,11},{8,4},{9,5},{1... | collective-permute-start | bytes 393224 | tf_op jit(solution)/shard_map/ppermute | solution.py:105
  6.0 24.3 %collective-permute-start.4 = (bf16[64,1024]{1,0:T(8,128)(2,1)}, bf16[64,1024]{1,0:T(8,128)(2,1)S(1)}, u32[]{:S(2)}, u32[]{:S(2)}) collective-permute-start(bf16[64,1024]{1,0:T(8,128)(2,1)} %bitcast.5), channel_id=1, source_target_pairs={{0,4},{1,5},{2,30},{3,31},{4,8},{5,9},{6,2},{7,3},{8,12},{9,13},{1... | collective-permute-start | bytes 393224 | tf_op jit(solution)/shard_map/ppermute | solution.py:105
  6.0 11.0 %collective-permute-start.1 = (bf16[64,1024]{1,0:T(8,128)(2,1)}, bf16[64,1024]{1,0:T(8,128)(2,1)S(1)}, u32[]{:S(2)}, u32[]{:S(2)}) collective-permute-start(bf16[64,1024]{1,0:T(8,128)(2,1)} %bitcast.7), channel_id=1, source_target_pairs={{0,1},{1,0},{2,3},{3,2},{4,5},{5,4},{6,7},{7,6},{8,9},{9,8},{10,11... | collective-permute-start | bytes 393224 | tf_op jit(solution)/shard_map/ppermute | solution.py:105
  8.4 3.9 %collective-permute-start = (bf16[3,32,64]{2,1,0:T(8,128)(2,1)S(1)}, bf16[3,32,64]{2,1,0:T(8,128)(2,1)S(1)}, u32[]{:S(2)}, u32[]{:S(2)}) collective-permute-start(bf16[3,32,64]{2,1,0:T(8,128)(2,1)S(1)} %reshape.6.refs_0_), channel_id=1, source_target_pairs={{0,1},{1,0},{2,3},{3,2},{4,5},{5,4},{6,7},{7,6},{8,9},{9,8},{10,11... | collective-permute-start | bytes 36872 | tf_op jit(solution)/shard_map/ppermute | solution.py:105
  12.4 15.9 %collective-permute-start.7 = (bf16[64,1024]{1,0:T(8,128)(2,1)}, bf16[64,1024]{1,0:T(8,128)(2,1)S(1)}, u32[]{:S(2)}, u32[]{:S(2)}) collective-permute-start(bf16[64,1024]{1,0:T(8,128)(2,1)} %bitcast.8), channel_id=1, source_target_pairs={{0,28},{1,29},{2,6},{3,7},{4,0},{5,1},{6,10},{7,11},{8,4},{9,5},{1... | collective-permute-start | bytes 393224 | tf_op jit(solution)/shard_map/ppermute | solution.py:105
  17.0 11.9 %collective-permute-start.9 = (bf16[64,1024]{1,0:T(8,128)(2,1)}, bf16[64,1024]{1,0:T(8,128)(2,1)S(1)}, u32[]{:S(2)}, u32[]{:S(2)}) collective-permute-start(bf16[64,1024]{1,0:T(8,128)(2,1)} %bitcast.9), channel_id=1, source_target_pairs={{0,4},{1,5},{2,30},{3,31},{4,8},{5,9},{6,2},{7,3},{8,12},{9,13},{1... | collective-permute-start | bytes 393224 | tf_op jit(solution)/shard_map/ppermute | solution.py:105
  17.1 21.3 %collective-permute-start.5 = (bf16[64,1024]{1,0:T(8,128)(2,1)}, bf16[64,1024]{1,0:T(8,128)(2,1)S(1)}, u32[]{:S(2)}, u32[]{:S(2)}) collective-permute-start(bf16[64,1024]{1,0:T(8,128)(2,1)} %bitcast.10), channel_id=1, source_target_pairs={{0,2},{1,3},{2,0},{3,1},{4,6},{5,7},{6,4},{7,5},{8,10},{9,11},{10,... | collective-permute-start | bytes 393224 | tf_op jit(solution)/shard_map/ppermute | solution.py:105
  17.1 0.9 %copy-start = (bf16[1,64,1024]{2,1,0:T(8,128)(2,1)S(1)}, bf16[1,64,1024]{2,1,0:T(8,128)(2,1)}, u32[]{:S(2)}) copy-start(bf16[1,64,1024]{2,1,0:T(8,128)(2,1)} %param.6) | copy-start | bytes 393220
  18.0 0.9 %copy-start.1 = (bf16[1,64,1024]{2,1,0:T(8,128)(2,1)S(1)}, bf16[1,64,1024]{2,1,0:T(8,128)(2,1)}, u32[]{:S(2)}) copy-start(bf16[1,64,1024]{2,1,0:T(8,128)(2,1)} %param.7) | copy-start | bytes 393220
  27.7 11.3 %collective-permute-start.6 = (bf16[64,1024]{1,0:T(8,128)(2,1)S(1)}, bf16[64,1024]{1,0:T(8,128)(2,1)S(1)}, u32[]{:S(2)}, u32[]{:S(2)}) collective-permute-start(bf16[64,1024]{1,0:T(8,128)(2,1)S(1)} %collective-permute-done.1.refs_3_), channel_id=1, source_target_pairs={{0,2},{1,3},{2,0},{3,1},{4,6},{5,7},{6,4},{7,5},{8,10},{9,11},{10,... | collective-permute-start | bytes 393224 | tf_op jit(solution)/shard_map/ppermute | solution.py:105
  28.2 10.7 %collective-permute-start.8 = (bf16[64,1024]{1,0:T(8,128)(2,1)S(1)}, bf16[64,1024]{1,0:T(8,128)(2,1)S(1)}, u32[]{:S(2)}, u32[]{:S(2)}) collective-permute-start(bf16[64,1024]{1,0:T(8,128)(2,1)S(1)} %collective-permute-done.7.refs_5_), channel_id=1, source_target_pairs={{0,1},{1,0},{2,3},{3,2},{4,5},{5,4},{6,7},{7,6},{8,9},{9,8},{10,11... | collective-permute-start | bytes 393224 | tf_op jit(solution)/shard_map/ppermute | solution.py:105
  28.9 10.0 %collective-permute-start.10 = (bf16[64,1024]{1,0:T(8,128)(2,1)S(1)}, bf16[64,1024]{1,0:T(8,128)(2,1)S(1)}, u32[]{:S(2)}, u32[]{:S(2)}) collective-permute-start(bf16[64,1024]{1,0:T(8,128)(2,1)S(1)} %collective-permute-done.9.refs_7_), channel_id=1, source_target_pairs={{0,1},{1,0},{2,3},{3,2},{4,5},{5,4},{6,7},{7,6},{8,9},{9,8},{10,11... | collective-permute-start | bytes 393224 | tf_op jit(solution)/shard_map/ppermute | solution.py:105
  30.3 10.8 %collective-permute-start.17 = (bf16[64,1024]{1,0:T(8,128)(2,1)S(1)}, bf16[64,1024]{1,0:T(8,128)(2,1)S(1)}, u32[]{:S(2)}, u32[]{:S(2)}) collective-permute-start(bf16[64,1024]{1,0:T(8,128)(2,1)S(1)} %collective-permute-done.3.refs_2_), channel_id=1, source_target_pairs={{0,2},{1,3},{2,0},{3,1},{4,6},{5,7},{6,4},{7,5},{8,10},{9,11},{10,... | collective-permute-start | bytes 393224 | tf_op jit(solution)/shard_map/ppermute | solution.py:105
  38.4 12.6 %collective-permute-start.18 = (bf16[64,1024]{1,0:T(8,128)(2,1)S(1)}, bf16[64,1024]{1,0:T(8,128)(2,1)S(1)}, u32[]{:S(2)}, u32[]{:S(2)}) collective-permute-start(bf16[64,1024]{1,0:T(8,128)(2,1)S(1)} %collective-permute-done.7.refs_5_), channel_id=1, source_target_pairs={{0,2},{1,3},{2,0},{3,1},{4,6},{5,7},{6,4},{7,5},{8,10},{9,11},{10,... | collective-permute-start | bytes 393224 | tf_op jit(solution)/shard_map/ppermute | solution.py:105
  40.3 17.2 %collective-permute-start.11 = (f32[3,32,64]{2,1,0:T(8,128)S(1)}, f32[3,32,64]{2,1,0:T(8,128)S(1)}, u32[]{:S(2)}, u32[]{:S(2)}) collective-permute-start(f32[3,32,64]{2,1,0:T(8,128)S(1)} %get-tuple-element.23), channel_id=1, source_target_pairs={{0,2},{1,3},{2,0},{3,1},{4,6},{5,7},{6,4},{7,5},{8,10},{9,11},{10,... | collective-permute-start | bytes 73736 | tf_op jit(solution)/shard_map/ppermute | solution.py:105
  40.4 17.3 %collective-permute-start.12 = (f32[3,32,64]{2,1,0:T(8,128)S(1)}, f32[3,32,64]{2,1,0:T(8,128)S(1)}, u32[]{:S(2)}, u32[]{:S(2)}) collective-permute-start(f32[3,32,64]{2,1,0:T(8,128)S(1)} %get-tuple-element.24), channel_id=1, source_target_pairs={{0,3},{1,2},{2,1},{3,0},{4,7},{5,6},{6,5},{7,4},{8,11},{9,10},{10,... | collective-permute-start | bytes 73736 | tf_op jit(solution)/shard_map/ppermute | solution.py:105
  41.1 17.3 %collective-permute-start.13 = (f32[3,32,64]{2,1,0:T(8,128)S(1)}, f32[3,32,64]{2,1,0:T(8,128)S(1)}, u32[]{:S(2)}, u32[]{:S(2)}) collective-permute-start(f32[3,32,64]{2,1,0:T(8,128)S(1)} %get-tuple-element.25), channel_id=1, source_target_pairs={{0,4},{1,5},{2,30},{3,31},{4,8},{5,9},{6,2},{7,3},{8,12},{9,13},{1... | collective-permute-start | bytes 73736 | tf_op jit(solution)/shard_map/ppermute | solution.py:105
  41.1 9.9 %collective-permute-start.19 = (bf16[64,1024]{1,0:T(8,128)(2,1)S(1)}, bf16[64,1024]{1,0:T(8,128)(2,1)S(1)}, u32[]{:S(2)}, u32[]{:S(2)}) collective-permute-start(bf16[64,1024]{1,0:T(8,128)(2,1)S(1)} %collective-permute-done.8.refs_6_), channel_id=1, source_target_pairs={{0,2},{1,3},{2,0},{3,1},{4,6},{5,7},{6,4},{7,5},{8,10},{9,11},{10,... | collective-permute-start | bytes 393224 | tf_op jit(solution)/shard_map/ppermute | solution.py:105
  51.0 11.9 %collective-permute-start.14 = (f32[3,32,64]{2,1,0:T(8,128)S(1)}, f32[3,32,64]{2,1,0:T(8,128)S(1)}, u32[]{:S(2)}, u32[]{:S(2)}) collective-permute-start(f32[3,32,64]{2,1,0:T(8,128)S(1)} %get-tuple-element.26), channel_id=1, source_target_pairs={{0,5},{1,4},{2,31},{3,30},{4,9},{5,8},{6,3},{7,2},{8,13},{9,12},{1... | collective-permute-start | bytes 73736 | tf_op jit(solution)/shard_map/ppermute | solution.py:105
  51.1 11.8 %collective-permute-start.15 = (f32[3,32,64]{2,1,0:T(8,128)S(1)}, f32[3,32,64]{2,1,0:T(8,128)S(1)}, u32[]{:S(2)}, u32[]{:S(2)}) collective-permute-start(f32[3,32,64]{2,1,0:T(8,128)S(1)} %get-tuple-element.27), channel_id=1, source_target_pairs={{0,28},{1,29},{2,6},{3,7},{4,0},{5,1},{6,10},{7,11},{8,4},{9,5},{1... | collective-permute-start | bytes 73736 | tf_op jit(solution)/shard_map/ppermute | solution.py:105
  57.5 5.4 %collective-permute-start.16 = (f32[3,32,64]{2,1,0:T(8,128)S(1)}, f32[3,32,64]{2,1,0:T(8,128)S(1)}, u32[]{:S(2)}, u32[]{:S(2)}) collective-permute-start(f32[3,32,64]{2,1,0:T(8,128)S(1)} %get-tuple-element.28), channel_id=1, source_target_pairs={{0,29},{1,28},{2,7},{3,6},{4,1},{5,0},{6,11},{7,10},{8,5},{9,4},{1... | collective-permute-start | bytes 73736 | tf_op jit(solution)/shard_map/ppermute | solution.py:105
  57.6 6.2 %collective-permute-start.20 = (f32[3,32,64]{2,1,0:T(8,128)S(1)}, f32[3,32,64]{2,1,0:T(8,128)S(1)}, u32[]{:S(2)}, u32[]{:S(2)}) collective-permute-start(f32[3,32,64]{2,1,0:T(8,128)S(1)} %get-tuple-element.31), channel_id=1, source_target_pairs={{0,30},{1,31},{2,4},{3,5},{4,2},{5,3},{6,8},{7,9},{8,6},{9,7},{10,... | collective-permute-start | bytes 73736 | tf_op jit(solution)/shard_map/ppermute | solution.py:105
  58.4 7.1 %collective-permute-start.21 = (f32[3,32,64]{2,1,0:T(8,128)S(1)}, f32[3,32,64]{2,1,0:T(8,128)S(1)}, u32[]{:S(2)}, u32[]{:S(2)}) collective-permute-start(f32[3,32,64]{2,1,0:T(8,128)S(1)} %get-tuple-element.32), channel_id=1, source_target_pairs={{0,31},{1,30},{2,5},{3,4},{4,3},{5,2},{6,9},{7,8},{8,7},{9,6},{10,... | collective-permute-start | bytes 73736 | tf_op jit(solution)/shard_map/ppermute | solution.py:105

commit v2 on v1

v2 whole, which is shorter than its diff:
```python
import functools

import jax
import jax.numpy as jnp
from jax import lax
from jax.experimental import pallas as pl
from jax.experimental.pallas import tpu as pltpu
from jax.sharding import PartitionSpec as P

BF16, F32 = jnp.bfloat16, jnp.float32
VMEM_SPEC = pl.BlockSpec(memory_space=pltpu.VMEM)
SMEM_SPEC = pl.BlockSpec(memory_space=pltpu.SMEM)
HBM_SPEC = pl.BlockSpec(memory_space=pltpu.HBM)
MIB = 1 << 20
NEAR, FAR, AHEAD, BEHIND = range(4)


def contract(left, right, left_dim, right_dim):
    dims = (((left_dim,), (right_dim,)), ((), ()))
    return lax.dot_general(left, right, dims, preferred_element_type=F32)


def screened_copy(screened, info, slot, part, cols, buffer, sem):
    count = screened.shape[2] // cols
    home = lax.rem(info[0] + part, count)
    columns = pl.ds(pl.multiple_of(home * cols, cols), cols)
    return pltpu.make_async_copy(
        screened.at[info[1 + slot], :, columns], buffer.at[:, pl.ds(part * cols, cols)], sem
    )


def first_kernel(count, later, info, *refs):
    vec_parts, con_parts = refs[:count], refs[count : 2 * count]
    bundle_home, bundle_near, screened = refs[2 * count : 2 * count + 3]
    pairs, folded = refs[2 * count + 3 : 2 * count + 5]
    weights = refs[2 * count + 5 : -3]
    vec_all, buffer, sems = refs[-3:]
    vec_count, rows, _ = vec_parts[0].shape
    cols = con_parts[0].shape[1]
    valence = vec_all.shape[1]
    slots, buffers = (NEAR,) + later, (buffer,) + tuple(weights)

    def copies(i):
        return [
            screened_copy(screened, info, slots[i], part, cols, buffers[i], sems.at[i, part])
            for part in range(count)
        ]

    for i in range(len(slots)):
        for copy in copies(i):
            copy.start()
    for part in range(count):
        offset = pl.multiple_of(lax.rem(info[0] + part, count) * rows, rows)
        for s in range(vec_count):
            vec_all[s, pl.ds(offset, rows), :] = vec_parts[part][s].astype(F32)
    for s in range(vec_count):
        half = contract(bundle_home[pl.ds(0, valence), :], vec_all[s].astype(BF16), 0, 0).astype(BF16)
        for part in range(count):
            pairs[s, :, pl.ds(part * cols, cols)] = contract(
                half, con_parts[part][...], 1, 0
            ).astype(BF16)
    for copy in copies(0):
        copy.wait()
    for s in range(vec_count):
        folded[pl.ds(s * valence, valence), :] = contract(
            bundle_near[pl.ds(0, valence), :], buffer[...] * pairs[s], 1, 0
        ).astype(BF16)
    for i in range(1, len(slots)):
        for copy in copies(i):
            copy.wait()


def fold_kernel(count, used, later, info, *refs):
    pairs = refs[0]
    bundles, weights = refs[1 : 1 + used], refs[1 + used : 1 + 2 * used]
    outs = refs[1 + 2 * used :]
    if later:
        screened, outs = outs[0], outs[2:-1]
    foldeds, nexts = outs[:used], outs[used:]
    vec_count, _, points = pairs.shape
    cols = points // count
    valence = foldeds[0].shape[0] // vec_count

    def copies(i):
        return [
            screened_copy(screened, info, later[i], part, cols, nexts[i], refs[-1].at[i, part])
            for part in range(count)
        ]

    for i in range(len(later)):
        for copy in copies(i):
            copy.start()
    for i in range(used):
        for s in range(vec_count):
            foldeds[i][pl.ds(s * valence, valence), :] = contract(
                bundles[i][pl.ds(0, valence), :], weights[i][...] * pairs[s], 1, 0
            ).astype(BF16)
    for i in range(len(later)):
        for copy in copies(i):
            copy.wait()


def result_kernel(count, info, *refs):
    foldeds, bundles = refs[:4], refs[4:8]
    others = refs[8 : 8 + 4 * (count - 1)]
    near, ahead, behind, work = refs[-4:]
    outs = (near.at[0], near.at[1], ahead, behind)
    _, vec_count, rows, _ = ahead.shape
    valence = foldeds[0].shape[0] // vec_count
    cols = bundles[0].shape[1]
    for i in range(4):
        total = contract(
            foldeds[i][:, pl.ds(0, cols)], bundles[i][pl.ds(valence, bundles[i].shape[0] - valence), :], 1, 1
        )
        for part in range(1, count):
            total += contract(
                foldeds[i][:, pl.ds(part * cols, cols)],
                others[i * (count - 1) + part - 1][...],
                1,
                1,
            )
        work[i] = total
        for part in range(count):
            offset = lax.rem(info[0] + part, count) * rows
            for s in range(vec_count):
                start = pl.multiple_of(s * valence + offset, 8)
                outs[i][part, s] = work[i, pl.ds(start, rows), :]


def moved(value, pairs_of):
    ka, mu = lax.axis_size("ka"), lax.axis_size("mu")
    pairs = []
    for k in range(ka):
        for m in range(mu):
            k_to, m_to = pairs_of(k, m)
            pairs.append((k * mu + m, (k_to % ka) * mu + m_to % mu))
    return lax.ppermute(value, ("ka", "mu"), pairs)


def target_of(slot, k):
    sign = 1 - 2 * (k % 2)
    return k + sign * {NEAR: 1, FAR: -1, AHEAD: 2, BEHIND: -2}[slot]


def local(vectors, phi_val, phi_con, screened, partner):
    del partner
    ka, count = lax.axis_size("ka"), lax.axis_size("mu")
    vec_count, local_k, local_pairs = vectors.shape
    _, valence, rows_m = phi_val.shape
    _, conduction, _ = phi_con.shape
    points = screened.shape[2]
    if local_k != 1 or ka % 2:
        raise ValueError("unsupported shapes")
    rows = local_pairs // conduction

    me, parity = lax.axis_index("mu"), lax.axis_index("ka") % 2
    info = jnp.concatenate([me[None], jnp.arange(4) ^ parity]).astype(jnp.int32)

    def from_slot(slot):
        back = {NEAR: NEAR, FAR: FAR, AHEAD: BEHIND, BEHIND: AHEAD}[slot]
        if slot in (AHEAD, BEHIND):
            return lambda k, m: (target_of(back, k), m)
        return lambda k, m: (target_of(slot, k), m)

    def over_mu(value):
        return [value] + [moved(value, lambda k, m, t=t: (k, m - t)) for t in range(1, count)]

    con_home = phi_con[0]
    bundle_home = jnp.concatenate([phi_val[0], con_home], axis=0)
    vec_home = vectors.astype(BF16).reshape(vec_count, rows, conduction)
    vec_home, bundle_home, con_home = lax.optimization_barrier((vec_home, bundle_home, con_home))
    vec_parts = over_mu(vec_home)
    con_parts = over_mu(con_home)
    bundle = {s: moved(bundle_home, from_slot(s)) for s in (NEAR, AHEAD, BEHIND)}
    bundle[FAR] = moved(bundle[AHEAD], from_slot(NEAR))
    others = {s: over_mu(bundle[s][valence:])[1:] for s in (AHEAD, BEHIND)}
    others[NEAR] = [moved(part, from_slot(NEAR)) for part in con_parts[1:]]
    others[FAR] = [moved(part, from_slot(NEAR)) for part in others[AHEAD]]

    pairs_type = jax.ShapeDtypeStruct((vec_count, rows_m, points), BF16)
    folded_type = jax.ShapeDtypeStruct((vec_count * valence, points), BF16)
    weight_type = jax.ShapeDtypeStruct((rows_m, points), BF16)
    fold_flops = 2 * vec_count * valence * rows_m * points

    def params(mib):
        return pltpu.CompilerParams(vmem_limit_bytes=mib * MIB)

    later = (AHEAD, BEHIND)
    first = pl.pallas_call(
        functools.partial(first_kernel, count, later),
        out_shape=[pairs_type, folded_type] + [weight_type] * len(later),
        in_specs=[SMEM_SPEC] + [VMEM_SPEC] * (2 * count + 2) + [HBM_SPEC],
        out_specs=[VMEM_SPEC] * (2 + len(later)),
        scratch_shapes=[
            pltpu.VMEM((vec_count, valence, conduction), F32),
            pltpu.VMEM((rows_m, points), BF16),
            pltpu.SemaphoreType.DMA((1 + len(later), count)),
        ],
        compiler_params=params(24),
        cost_estimate=pl.CostEstimate(flops=8 * fold_flops, bytes_accessed=4 * MIB, transcendentals=0),
        name="first",
    )
    pairs, folded_near, *weights = first(
        info, *vec_parts, *con_parts, bundle_home, bundle[NEAR], screened
    )

    def fold(pairs, weights, slots, later):
        used = len(slots)
        extra = len(later)
        out = pl.pallas_call(
            functools.partial(fold_kernel, count, used, later),
            out_shape=[pairs_type] * bool(extra)
            + [folded_type] * used
            + [weight_type] * extra,
            in_specs=[SMEM_SPEC]
            + [VMEM_SPEC] * (1 + 2 * used)
            + [HBM_SPEC] * bool(extra),
            out_specs=[VMEM_SPEC] * (bool(extra) + used + extra),
            scratch_shapes=[pltpu.SemaphoreType.DMA((extra, count))] * bool(extra),
            input_output_aliases={1: 0} if extra else {},
            compiler_params=params(20),
            cost_estimate=pl.CostEstimate(
                flops=4 * used * fold_flops, bytes_accessed=4 * used * MIB, transcendentals=0
            ),
        )(info, pairs, *[bundle[s] for s in slots], *weights, *[screened] * bool(extra))
        if extra:
            pairs, out = out[0], out[1:]
        return pairs, out[:used], out[used:]

    pairs, (folded_ahead, folded_behind), weights = fold(pairs, weights, (AHEAD, BEHIND), (FAR,))
    _, (folded_far,), _ = fold(pairs, weights, (FAR,), ())

    result = (count, vec_count, rows, conduction)
    order = (NEAR, FAR, AHEAD, BEHIND)
    near, ahead, behind = pl.pallas_call(
        functools.partial(result_kernel, count),
        out_shape=[jax.ShapeDtypeStruct(s, F32) for s in ((2,) + result, result, result)],
        in_specs=[SMEM_SPEC] + [VMEM_SPEC] * (4 + 4 * count),
        out_specs=[VMEM_SPEC] * 3,
        scratch_shapes=[pltpu.VMEM((4, vec_count * valence, conduction), F32)],
        compiler_params=params(10),
        cost_estimate=pl.CostEstimate(flops=fold_flops, bytes_accessed=MIB, transcendentals=0),
        name="result",
    )(
        info,
        folded_near,
        folded_far,
        folded_ahead,
        folded_behind,
        *[bundle[s] for s in order],
        *[part for s in order for part in others[s]],
    )
    near = moved(near, lambda k, m: (target_of(NEAR, k), m))
    shared = jnp.stack([near[0], ahead + near[1], behind])
    summed = shared[:, 0]
    for part in range(1, count):
        summed += moved(shared[:, part], lambda k, m, part=part: (k, m + part))
    total = summed[0]
    for i, slot in ((1, AHEAD), (2, BEHIND)):
        total += moved(summed[i], lambda k, m, slot=slot: (target_of(slot, k), m))
    return total.reshape(vec_count, 1, local_pairs)


def solution(mesh):
    placed = (
        P(None, "ka", "mu"),
        P("ka", None, "mu"),
        P("ka", None, "mu"),
        P(None, "mu", None),
        P("ka", None),
    )

    return jax.shard_map(
        local, mesh=mesh, in_specs=placed, out_specs=P(None, "ka", "mu"), check_vma=False
    )
```

time: 66.5 us -> 60.5 us (0.910)
  starting transfers between devices: 32.2 us -> 18.5 us
  waiting for transfers between devices: 5.99 us -> 17.6 us
  Pallas kernels: 24.4 us -> 20.4 us
  other arithmetic: 0.92 us -> 1.95 us
  local copies, waits for them, and re-layouts: 2.6 us -> 1.74 us
    ppermute x22 -> x14, starting transfers between devices: 32.2 us -> 18.5 us  [moved(): return lax.ppermute(value, ('ka', 'mu'), pairs)]
    ppermute x22 -> x14, waiting for transfers between devices: 5.99 us -> 17.6 us  [moved(): return lax.ppermute(value, ('ka', 'mu'), pairs)]
    pallas_call x5 -> x4, Pallas kernels: 24.4 us -> 20.4 us  [the longest x2 10.1 us: fold(): pl.pallas_call(functools.partial(fold_kernel, count, used, later), out_sh...]
    concatenate x0 -> x1, other arithmetic: none -> 0.99 us  [local(): bundle_home = jnp.concatenate([phi_val[0], con_home], axis=0)]
    unnamed x4 -> x2, local copies, waits for them, and re-layouts: 1.8 us -> 0.9 us
  transfers between devices with their start and end apart: 22 -> 14, of which waited for: 3 -> 5; matrix products, arithmetic and copies ran while one was open for 1% -> 0% of each run, Pallas kernels for 37% -> 31%
where the time goes in v2:
time: 60.5 us; the launch traced here: 60.3 us
  Pallas kernels  20.4 us (34%)
  starting transfers between devices  18.5 us (31%)
  waiting for transfers between devices  17.6 us (29%)
  other arithmetic  1.95 us (3%)
  local copies, waits for them, and re-layouts  1.74 us (3%)
    ppermute x14, starting transfers between devices, moved(): return lax.ppermute(value, ('ka', 'mu'), pairs)  18.5 us
    ppermute x14, waiting for transfers between devices, moved(): return lax.ppermute(value, ('ka', 'mu'), pairs)  17.6 us
    pallas_call x2, Pallas kernels, fold(): pl.pallas_call(functools.partial(fold_kernel, count, used, later), out_sh...  10.1 us
    pallas_call x1, Pallas kernels, local(): first(info, *vec_parts, *con_parts, bundle_home, bundle[NEAR], screened)  8.77 us
    pallas_call x1, Pallas kernels, local(): pl.pallas_call(functools.partial(result_kernel, count), out_shape=[jax.Sh...  1.55 us
  transfers between devices with their start and end apart: 14, of which 5 were waited for; matrix products, arithmetic and copies ran while one was open for 0% of the time, Pallas kernels for 31%

profile of v2, /device:TPU:0, one launch (start us, length us, event | category | flops | bytes accessed | tf_op | source)
XLA Modules:
  0.0 60.3 jit_solution(1233694720041668129)
XLA Ops:
  0.0 0.8 %convert_reduce_fusion = bf16[3,2048]{1,0:T(4,128)(2,1)S(1)} fusion(f32[3,1,2048]{2,1,0:T(1,128)} %param.5), kind=kLoop, calls=%fused_computation.13 | loop fusion | flops 6144 | bytes 36864 | tf_op jit(solution)/shard_map/convert_element_type | solution.py:170
  0.8 0.1 reshape.6.refs_0_
  0.9 1.0 %pad_maximum_fusion.1.refs_4_ = bf16[128,1024]{1,0:T(8,128)(2,1)S(1)} fusion(bf16[64,1024]{1,0:T(8,128)(2,1)} %bitcast.30, bf16[64,1024]{1,0:T(8,128)(2,1)} %bitcast.34), kind=kLoop, calls=%fused_computation.1 | loop fusion | flops 524288 | bytes 524288 | tf_op jit(solution)/shard_map/concatenate | solution.py:169
  1.9 6.1 %collective-permute-start.3 = (bf16[128,1024]{1,0:T(8,128)(2,1)S(1)}, bf16[128,1024]{1,0:T(8,128)(2,1)S(1)}, u32[]{:S(2)}, u32[]{:S(2)}) collective-permute-start(bf16[128,1024]{1,0:T(8,128)(2,1)S(1)} %pad_maximum_fusion.1.refs_4_), channel_id=1, source_target_pairs={{0,28},{1,29},{2,6},{3,7},{4,0},{5,1},{6,10},{7,11},{8,4},{9,5},{1... | collective-permute-start | bytes 786440 | tf_op jit(solution)/shard_map/ppermute | solution.py:137
  8.0 0.0 collective-permute-start.4
  8.0 0.0 collective-permute-start.2
  8.0 1.5 %collective-permute-start = (bf16[3,32,64]{2,1,0:T(8,128)(2,1)S(1)}, bf16[3,32,64]{2,1,0:T(8,128)(2,1)S(1)}, u32[]{:S(2)}, u32[]{:S(2)}) collective-permute-start(bf16[3,32,64]{2,1,0:T(8,128)(2,1)S(1)} %reshape.6.refs_0_), channel_id=1, source_target_pairs={{0,1},{1,0},{2,3},{3,2},{4,5},{5,4},{6,7},{7,6},{8,9},{9,8},{10,11... | collective-permute-start | bytes 36872 | tf_op jit(solution)/shard_map/ppermute | solution.py:137
  9.5 0.5 collective-permute-start.1
  10.0 0.1 pad_add_fusion.info
  10.1 5.3 %collective-permute-done.1.refs_3_ = bf16[64,1024]{1,0:T(8,128)(2,1)S(1)} collective-permute-done((bf16[64,1024]{1,0:T(8,128)(2,1)}, bf16[64,1024]{1,0:T(8,128)(2,1)S(1)}, u32[]{:S(2)}, u32[]{:S(2)}) %collective-permute-start.1) | collective-permute-done | bytes 131104 | tf_op jit(solution)/shard_map/ppermute | solution.py:137
  15.3 0.0 collective-permute-start.6
  15.3 0.0 collective-permute-done.3.refs_1_.refs_6_
  15.3 4.4 %collective-permute-start.7 = (bf16[64,1024]{1,0:T(8,128)(2,1)S(1)}, bf16[64,1024]{1,0:T(8,128)(2,1)S(1)}, u32[]{:S(2)}, u32[]{:S(2)}) collective-permute-start(bf16[64,1024]{1,0:T(8,128)(2,1)S(1)} %slice.36), channel_id=1, source_target_pairs={{0,1},{1,0},{2,3},{3,2},{4,5},{5,4},{6,7},{7,6},{8,9},{9,8},{10,11... | collective-permute-start | bytes 393224 | tf_op jit(solution)/shard_map/ppermute | solution.py:137
  19.7 0.0 collective-permute-done.4.refs_2_.refs_7_
  19.8 0.1 collective-permute-start.9
  19.9 0.0 collective-permute-done.refs_1_
  19.9 0.1 collective-permute-start.5
  19.9 0.0 collective-permute-done.2.refs_5_.refs_4_
  19.9 0.0 copy-start
  20.0 0.9 %copy-done = bf16[1,64,1024]{2,1,0:T(8,128)(2,1)S(1)} copy-done((bf16[1,64,1024]{2,1,0:T(8,128)(2,1)S(1)}, bf16[1,64,1024]{2,1,0:T(8,128)(2,1)}, u32[]{:S(2)}) %copy-start) | copy-done | bytes 131096
  20.9 8.8 %first.1 = (bf16[3,1024,2048]{2,1,0:T(8,128)(2,1)S(1)}, bf16[192,2048]{1,0:T(8,128)(2,1)S(1)}, bf16[1024,2048]{1,0:T(8,128)(2,1)S(1)}, bf16[1024,2048]{1,0:T(8,128)(2,1)S(1)}) custom-call(s32[5]{0:T(128)S(1)} %pad_add_fusion.info, bf16[3,32,64]{2,1,0:T(8,128)(2,1)S(1)} %reshape.6.refs_0_, bf16[3,32,64]{2,1,0:T(8,128)(2,1)S(1)} %collective-permute-done.refs_1_, ...), custom_call_target="tpu_custom_call" | custom-call | flops 6442450944 | bytes 4194304 | tf_op jit(solution)/shard_map/first/pallas_call | solution.py:203
  29.6 7.2 %shard_map.46 = (bf16[3,1024,2048]{2,1,0:T(8,128)(2,1)S(1)}, bf16[192,2048]{1,0:T(8,128)(2,1)S(1)}, bf16[192,2048]{1,0:T(8,128)(2,1)S(1)}, bf16[1024,2048]{1,0:T(8,128)(2,1)S(1)}) custom-call(s32[5]{0:T(128)S(1)} %pad_add_fusion.info, bf16[3,1024,2048]{2,1,0:T(8,128)(2,1)S(1)} %get-tuple-element.23.refs_0_, ...), custom_call_target="tpu_custom_call", output_to_operand_aliasing={{0}: (1, {})} | custom-call | flops 6442450944 | bytes 8388608 | tf_op jit(solution)/shard_map/pallas_call | solution.py:210
  36.8 0.0 collective-permute-done.7.refs_10_
  36.9 0.6 collective-permute-start.8
  37.4 0.0 collective-permute-done.5.refs_1_.refs_5_
  37.4 2.8 %shard_map.47.refs_1_ = bf16[192,2048]{1,0:T(8,128)(2,1)S(1)} custom-call(s32[5]{0:T(128)S(1)} %pad_add_fusion.info, bf16[3,1024,2048]{2,1,0:T(8,128)(2,1)S(1)} %get-tuple-element.26.refs_0_, bf16[128,1024]{1,0:T(8,128)(2,1)S(1)} %collective-permute-done.5.refs_1_.refs_5_, bf16[1024,2048]{1,0:T(8,128)(2,1)S(1)} %get-tuple-element.27.refs_2_), custom_call_target="tpu_custom_call" | custom-call | flops 3221225472 | bytes 4194304 | tf_op jit(solution)/shard_map/pallas_call | solution.py:210
  40.3 0.0 collective-permute-done.6.refs_8_
  40.3 0.0 collective-permute-done.9.refs_11_
  40.3 0.0 collective-permute-done.8.refs_9_
  40.3 1.6 %result.1 = (f32[2,2,3,32,64]{4,3,2,1,0:T(8,128)S(1)}, f32[2,3,32,64]{3,2,1,0:T(8,128)S(1)}, f32[2,3,32,64]{3,2,1,0:T(8,128)S(1)}) custom-call(s32[5]{0:T(128)S(1)} %pad_add_fusion.info, bf16[192,2048]{1,0:T(8,128)(2,1)S(1)} %get-tuple-element.22.refs_0_, bf16[192,2048]{1,0:T(8,128)(2,1)S(1)} %shard_map.47.refs_1_, ...), custom_call_target="tpu_custom_call" | custom-call | flops 805306368 | bytes 1048576 | tf_op jit(solution)/shard_map/result/pallas_call | solution.py:235
  41.9 0.1 collective-permute-start.10
  42.0 1.4 %collective-permute-done.10 = f32[2,2,3,32,64]{4,3,2,1,0:T(8,128)S(1)} collective-permute-done((f32[2,2,3,32,64]{4,3,2,1,0:T(8,128)S(1)}, f32[2,2,3,32,64]{4,3,2,1,0:T(8,128)S(1)}, u32[]{:S(2)}, u32[]{:S(2)}) %collective-permute-start.10) | collective-permute-done | bytes 98336 | tf_op jit(solution)/shard_map/ppermute | solution.py:137
  43.4 2.0 %collective-permute-start.11 = (f32[3,3,32,64]{3,2,1,0:T(8,128)S(1)}, f32[3,3,32,64]{3,2,1,0:T(8,128)S(1)}, u32[]{:S(2)}, u32[]{:S(2)}) collective-permute-start(f32[3,3,32,64]{3,2,1,0:T(8,128)S(1)} %slice_bitcast_fusion), channel_id=1, source_target_pairs={{0,1},{1,0},{2,3},{3,2},{4,5},{5,4},{6,7},{7,6},{8,9},{9,8},{10,11... | collective-permute-start | bytes 221192 | tf_op jit(solution)/shard_map/ppermute | solution.py:137
  45.5 4.1 %collective-permute-done.11 = f32[3,3,32,64]{3,2,1,0:T(8,128)S(1)} collective-permute-done((f32[3,3,32,64]{3,2,1,0:T(8,128)S(1)}, f32[3,3,32,64]{3,2,1,0:T(8,128)S(1)}, u32[]{:S(2)}, u32[]{:S(2)}) %collective-permute-start.11) | collective-permute-done | bytes 73760 | tf_op jit(solution)/shard_map/ppermute | solution.py:137
  49.6 3.1 %collective-permute-start.13 = (f32[3,32,64]{2,1,0:T(8,128)S(1)}, f32[3,32,64]{2,1,0:T(8,128)S(1)}, u32[]{:S(2)}, u32[]{:S(2)}) collective-permute-start(f32[3,32,64]{2,1,0:T(8,128)S(1)} %get-tuple-element.34), channel_id=1, source_target_pairs={{0,28},{1,29},{2,6},{3,7},{4,0},{5,1},{6,10},{7,11},{8,4},{9,5},{1... | collective-permute-start | bytes 73736 | tf_op jit(solution)/shard_map/ppermute | solution.py:137
  52.8 0.0 collective-permute-start.12
  52.8 2.0 %collective-permute-done.13 = f32[3,32,64]{2,1,0:T(8,128)S(1)} collective-permute-done((f32[3,32,64]{2,1,0:T(8,128)S(1)}, f32[3,32,64]{2,1,0:T(8,128)S(1)}, u32[]{:S(2)}, u32[]{:S(2)}) %collective-permute-start.13) | collective-permute-done | bytes 24608 | tf_op jit(solution)/shard_map/ppermute | solution.py:137
  54.8 4.8 %collective-permute-done.12 = f32[3,32,64]{2,1,0:T(8,128)S(1)} collective-permute-done((f32[3,32,64]{2,1,0:T(8,128)S(1)}, f32[3,32,64]{2,1,0:T(8,128)S(1)}, u32[]{:S(2)}, u32[]{:S(2)}) %collective-permute-start.12) | collective-permute-done | bytes 24608 | tf_op jit(solution)/shard_map/ppermute | solution.py:137
  59.6 0.7 %reshape.8 = f32[3,1,2048]{2,1,0:T(1,128)} reshape(f32[3,32,64]{2,1,0:T(8,128)S(1)} %fusion.4) | data formatting | bytes 49152 | tf_op jit(solution)/shard_map/reshape | solution.py:261
  (10 shorter events, 0.1 us)
Async XLA Ops:
  1.9 13.4 %collective-permute-start.3 = (bf16[128,1024]{1,0:T(8,128)(2,1)S(1)}, bf16[128,1024]{1,0:T(8,128)(2,1)S(1)}, u32[]{:S(2)}, u32[]{:S(2)}) collective-permute-start(bf16[128,1024]{1,0:T(8,128)(2,1)S(1)} %pad_maximum_fusion.1.refs_4_), channel_id=1, source_target_pairs={{0,28},{1,29},{2,6},{3,7},{4,0},{5,1},{6,10},{7,11},{8,4},{9,5},{1... | collective-permute-start | bytes 786440 | tf_op jit(solution)/shard_map/ppermute | solution.py:137
  8.0 11.8 %collective-permute-start.4 = (bf16[128,1024]{1,0:T(8,128)(2,1)S(1)}, bf16[128,1024]{1,0:T(8,128)(2,1)S(1)}, u32[]{:S(2)}, u32[]{:S(2)}) collective-permute-start(bf16[128,1024]{1,0:T(8,128)(2,1)S(1)} %pad_maximum_fusion.1.refs_4_), channel_id=1, source_target_pairs={{0,4},{1,5},{2,30},{3,31},{4,8},{5,9},{6,2},{7,3},{8,12},{9,13},{1... | collective-permute-start | bytes 786440 | tf_op jit(solution)/shard_map/ppermute | solution.py:137
  8.0 12.0 %collective-permute-start.2 = (bf16[128,1024]{1,0:T(8,128)(2,1)S(1)}, bf16[128,1024]{1,0:T(8,128)(2,1)S(1)}, u32[]{:S(2)}, u32[]{:S(2)}) collective-permute-start(bf16[128,1024]{1,0:T(8,128)(2,1)S(1)} %pad_maximum_fusion.1.refs_4_), channel_id=1, source_target_pairs={{0,2},{1,3},{2,0},{3,1},{4,6},{5,7},{6,4},{7,5},{8,10},{9,11},{10,... | collective-permute-start | bytes 786440 | tf_op jit(solution)/shard_map/ppermute | solution.py:137
  8.0 11.9 %collective-permute-start = (bf16[3,32,64]{2,1,0:T(8,128)(2,1)S(1)}, bf16[3,32,64]{2,1,0:T(8,128)(2,1)S(1)}, u32[]{:S(2)}, u32[]{:S(2)}) collective-permute-start(bf16[3,32,64]{2,1,0:T(8,128)(2,1)S(1)} %reshape.6.refs_0_), channel_id=1, source_target_pairs={{0,1},{1,0},{2,3},{3,2},{4,5},{5,4},{6,7},{7,6},{8,9},{9,8},{10,11... | collective-permute-start | bytes 36872 | tf_op jit(solution)/shard_map/ppermute | solution.py:137
  9.5 5.8 %collective-permute-start.1 = (bf16[64,1024]{1,0:T(8,128)(2,1)}, bf16[64,1024]{1,0:T(8,128)(2,1)S(1)}, u32[]{:S(2)}, u32[]{:S(2)}) collective-permute-start(bf16[64,1024]{1,0:T(8,128)(2,1)} %bitcast.31), channel_id=1, source_target_pairs={{0,1},{1,0},{2,3},{3,2},{4,5},{5,4},{6,7},{7,6},{8,9},{9,8},{10,11... | collective-permute-start | bytes 393224 | tf_op jit(solution)/shard_map/ppermute | solution.py:137
  15.3 24.9 %collective-permute-start.6 = (bf16[64,1024]{1,0:T(8,128)(2,1)S(1)}, bf16[64,1024]{1,0:T(8,128)(2,1)S(1)}, u32[]{:S(2)}, u32[]{:S(2)}) collective-permute-start(bf16[64,1024]{1,0:T(8,128)(2,1)S(1)} %collective-permute-done.1.refs_3_), channel_id=1, source_target_pairs={{0,2},{1,3},{2,0},{3,1},{4,6},{5,7},{6,4},{7,5},{8,10},{9,11},{10,... | collective-permute-start | bytes 393224 | tf_op jit(solution)/shard_map/ppermute | solution.py:137
  15.3 21.5 %collective-permute-start.7 = (bf16[64,1024]{1,0:T(8,128)(2,1)S(1)}, bf16[64,1024]{1,0:T(8,128)(2,1)S(1)}, u32[]{:S(2)}, u32[]{:S(2)}) collective-permute-start(bf16[64,1024]{1,0:T(8,128)(2,1)S(1)} %slice.36), channel_id=1, source_target_pairs={{0,1},{1,0},{2,3},{3,2},{4,5},{5,4},{6,7},{7,6},{8,9},{9,8},{10,11... | collective-permute-start | bytes 393224 | tf_op jit(solution)/shard_map/ppermute | solution.py:137
  19.8 20.5 %collective-permute-start.9 = (bf16[64,1024]{1,0:T(8,128)(2,1)S(1)}, bf16[64,1024]{1,0:T(8,128)(2,1)S(1)}, u32[]{:S(2)}, u32[]{:S(2)}) collective-permute-start(bf16[64,1024]{1,0:T(8,128)(2,1)S(1)} %slice.37), channel_id=1, source_target_pairs={{0,1},{1,0},{2,3},{3,2},{4,5},{5,4},{6,7},{7,6},{8,9},{9,8},{10,11... | collective-permute-start | bytes 393224 | tf_op jit(solution)/shard_map/ppermute | solution.py:137
  19.9 17.6 %collective-permute-start.5 = (bf16[128,1024]{1,0:T(8,128)(2,1)S(1)}, bf16[128,1024]{1,0:T(8,128)(2,1)S(1)}, u32[]{:S(2)}, u32[]{:S(2)}) collective-permute-start(bf16[128,1024]{1,0:T(8,128)(2,1)S(1)} %collective-permute-done.3.refs_1_.refs_6_), channel_id=1, source_target_pairs={{0,2},{1,3},{2,0},{3,1},{4,6},{5,7},{6,4},{7,5},{8,10},{9,11},{10,... | collective-permute-start | bytes 786440 | tf_op jit(solution)/shard_map/ppermute | solution.py:137
  19.9 0.9 %copy-start = (bf16[1,64,1024]{2,1,0:T(8,128)(2,1)S(1)}, bf16[1,64,1024]{2,1,0:T(8,128)(2,1)}, u32[]{:S(2)}) copy-start(bf16[1,64,1024]{2,1,0:T(8,128)(2,1)} %param.7) | copy-start | bytes 393220
  36.9 3.4 %collective-permute-start.8 = (bf16[64,1024]{1,0:T(8,128)(2,1)S(1)}, bf16[64,1024]{1,0:T(8,128)(2,1)S(1)}, u32[]{:S(2)}, u32[]{:S(2)}) collective-permute-start(bf16[64,1024]{1,0:T(8,128)(2,1)S(1)} %collective-permute-done.7.refs_10_), channel_id=1, source_target_pairs={{0,2},{1,3},{2,0},{3,1},{4,6},{5,7},{6,4},{7,5},{8,10},{9,11},{10,... | collective-permute-start | bytes 393224 | tf_op jit(solution)/shard_map/ppermute | solution.py:137
  41.9 1.5 %collective-permute-start.10 = (f32[2,2,3,32,64]{4,3,2,1,0:T(8,128)S(1)}, f32[2,2,3,32,64]{4,3,2,1,0:T(8,128)S(1)}, u32[]{:S(2)}, u32[]{:S(2)}) collective-permute-start(f32[2,2,3,32,64]{4,3,2,1,0:T(8,128)S(1)} %get-tuple-element.30), channel_id=1, source_target_pairs={{0,2},{1,3},{2,0},{3,1},{4,6},{5,7},{6,4},{7,5},{8,10},{9,11},{10,... | collective-permute-start | bytes 294920 | tf_op jit(solution)/shard_map/ppermute | solution.py:137
  43.4 6.2 %collective-permute-start.11 = (f32[3,3,32,64]{3,2,1,0:T(8,128)S(1)}, f32[3,3,32,64]{3,2,1,0:T(8,128)S(1)}, u32[]{:S(2)}, u32[]{:S(2)}) collective-permute-start(f32[3,3,32,64]{3,2,1,0:T(8,128)S(1)} %slice_bitcast_fusion), channel_id=1, source_target_pairs={{0,1},{1,0},{2,3},{3,2},{4,5},{5,4},{6,7},{7,6},{8,9},{9,8},{10,11... | collective-permute-start | bytes 221192 | tf_op jit(solution)/shard_map/ppermute | solution.py:137
  49.6 5.1 %collective-permute-start.13 = (f32[3,32,64]{2,1,0:T(8,128)S(1)}, f32[3,32,64]{2,1,0:T(8,128)S(1)}, u32[]{:S(2)}, u32[]{:S(2)}) collective-permute-start(f32[3,32,64]{2,1,0:T(8,128)S(1)} %get-tuple-element.34), channel_id=1, source_target_pairs={{0,28},{1,29},{2,6},{3,7},{4,0},{5,1},{6,10},{7,11},{8,4},{9,5},{1... | collective-permute-start | bytes 73736 | tf_op jit(solution)/shard_map/ppermute | solution.py:137
  52.8 6.8 %collective-permute-start.12 = (f32[3,32,64]{2,1,0:T(8,128)S(1)}, f32[3,32,64]{2,1,0:T(8,128)S(1)}, u32[]{:S(2)}, u32[]{:S(2)}) collective-permute-start(f32[3,32,64]{2,1,0:T(8,128)S(1)} %get-tuple-element.33), channel_id=1, source_target_pairs={{0,4},{1,5},{2,30},{3,31},{4,8},{5,9},{6,2},{7,3},{8,12},{9,13},{1... | collective-permute-start | bytes 73736 | tf_op jit(solution)/shard_map/ppermute | solution.py:137

commit v3 on v2

--- a/solution.py
+++ b/solution.py
@@ -30,14 +30,14 @@
 
 
 def first_kernel(count, later, info, *refs):
-    vec_parts, con_parts = refs[:count], refs[count : 2 * count]
-    bundle_home, bundle_near, screened = refs[2 * count : 2 * count + 3]
-    pairs, folded = refs[2 * count + 3 : 2 * count + 5]
-    weights = refs[2 * count + 5 : -3]
+    vec_parts, con_others = refs[:count], refs[count : 2 * count - 1]
+    bundle_home, bundle_near, screened = refs[2 * count - 1 : 2 * count + 2]
+    pairs, folded = refs[2 * count + 2 : 2 * count + 4]
+    weights = refs[2 * count + 4 : -3]
     vec_all, buffer, sems = refs[-3:]
     vec_count, rows, _ = vec_parts[0].shape
-    cols = con_parts[0].shape[1]
-    valence = vec_all.shape[1]
+    cols = bundle_home.shape[1]
+    _, valence, conduction = vec_all.shape
     slots, buffers = (NEAR,) + later, (buffer,) + tuple(weights)
 
     def copies(i):
@@ -53,12 +53,13 @@
         offset = pl.multiple_of(lax.rem(info[0] + part, count) * rows, rows)
         for s in range(vec_count):
             vec_all[s, pl.ds(offset, rows), :] = vec_parts[part][s].astype(F32)
+    val_points = jnp.transpose(bundle_home[pl.ds(0, valence), :])
     for s in range(vec_count):
-        half = contract(bundle_home[pl.ds(0, valence), :], vec_all[s].astype(BF16), 0, 0).astype(BF16)
+        vec = vec_all[s].astype(BF16)
         for part in range(count):
-            pairs[s, :, pl.ds(part * cols, cols)] = contract(
-                half, con_parts[part][...], 1, 0
-            ).astype(BF16)
+            con = con_others[part - 1][...] if part else bundle_home[pl.ds(valence, conduction), :]
+            blended = contract(vec, con, 1, 0).astype(BF16)
+            pairs[s, :, pl.ds(part * cols, cols)] = contract(val_points, blended, 1, 0).astype(BF16)
     for copy in copies(0):
         copy.wait()
     for s in range(vec_count):
@@ -103,9 +104,9 @@
 def result_kernel(count, info, *refs):
     foldeds, bundles = refs[:4], refs[4:8]
     others = refs[8 : 8 + 4 * (count - 1)]
-    near, ahead, behind, work = refs[-4:]
-    outs = (near.at[0], near.at[1], ahead, behind)
-    _, vec_count, rows, _ = ahead.shape
+    near, far, behind, work = refs[-4:]
+    outs = (near.at[0], far, near.at[1], behind)
+    _, vec_count, rows, _ = far.shape
     valence = foldeds[0].shape[0] // vec_count
     cols = bundles[0].shape[1]
     for i in range(4):
@@ -166,9 +167,9 @@
         return [value] + [moved(value, lambda k, m, t=t: (k, m - t)) for t in range(1, count)]
 
     con_home = phi_con[0]
+    vec_home = vectors.astype(BF16).reshape(vec_count, rows, conduction)
+    vec_home, con_home = lax.optimization_barrier((vec_home, con_home))
     bundle_home = jnp.concatenate([phi_val[0], con_home], axis=0)
-    vec_home = vectors.astype(BF16).reshape(vec_count, rows, conduction)
-    vec_home, bundle_home, con_home = lax.optimization_barrier((vec_home, bundle_home, con_home))
     vec_parts = over_mu(vec_home)
     con_parts = over_mu(con_home)
     bundle = {s: moved(bundle_home, from_slot(s)) for s in (NEAR, AHEAD, BEHIND)}
@@ -189,7 +190,7 @@
     first = pl.pallas_call(
         functools.partial(first_kernel, count, later),
         out_shape=[pairs_type, folded_type] + [weight_type] * len(later),
-        in_specs=[SMEM_SPEC] + [VMEM_SPEC] * (2 * count + 2) + [HBM_SPEC],
+        in_specs=[SMEM_SPEC] + [VMEM_SPEC] * (2 * count + 1) + [HBM_SPEC],
         out_specs=[VMEM_SPEC] * (2 + len(later)),
         scratch_shapes=[
             pltpu.VMEM((vec_count, valence, conduction), F32),
@@ -201,7 +202,7 @@
         name="first",
     )
     pairs, folded_near, *weights = first(
-        info, *vec_parts, *con_parts, bundle_home, bundle[NEAR], screened
+        info, *vec_parts, *con_parts[1:], bundle_home, bundle[NEAR], screened
     )
 
     def fold(pairs, weights, slots, later):
@@ -232,7 +233,7 @@
 
     result = (count, vec_count, rows, conduction)
     order = (NEAR, FAR, AHEAD, BEHIND)
-    near, ahead, behind = pl.pallas_call(
+    near, far, behind = pl.pallas_call(
         functools.partial(result_kernel, count),
         out_shape=[jax.ShapeDtypeStruct(s, F32) for s in ((2,) + result, result, result)],
         in_specs=[SMEM_SPEC] + [VMEM_SPEC] * (4 + 4 * count),
@@ -251,13 +252,14 @@
         *[part for s in order for part in others[s]],
     )
     near = moved(near, lambda k, m: (target_of(NEAR, k), m))
-    shared = jnp.stack([near[0], ahead + near[1], behind])
+    shared = jnp.stack([near[0], far + near[1], behind])
     summed = shared[:, 0]
     for part in range(1, count):
-        summed += moved(shared[:, part], lambda k, m, part=part: (k, m + part))
-    total = summed[0]
-    for i, slot in ((1, AHEAD), (2, BEHIND)):
-        total += moved(summed[i], lambda k, m, slot=slot: (target_of(slot, k), m))
+        sent = shared[:, part].astype(BF16)
+        summed += moved(sent, lambda k, m, part=part: (k, m + part)).astype(F32)
+    arrived = moved(summed[1:].astype(BF16), lambda k, m: (target_of(BEHIND, k), m))
+    from_near = moved(arrived[0], lambda k, m: (target_of(NEAR, k), m))
+    total = summed[0] + arrived[1].astype(F32) + from_near.astype(F32)
     return total.reshape(vec_count, 1, local_pairs)
 
 

time: 60.5 us -> 54.4 us (0.90)
  waiting for transfers between devices: 17.6 us -> 11 us
  starting transfers between devices: 18.5 us -> 19.7 us
  local copies, waits for them, and re-layouts: 1.74 us -> 0.85 us
    ppermute x14, waiting for transfers between devices: 17.6 us -> 11 us  [moved(): return lax.ppermute(value, ('ka', 'mu'), pairs)]
    ppermute x14, starting transfers between devices: 18.5 us -> 19.7 us  [moved(): return lax.ppermute(value, ('ka', 'mu'), pairs)]
    unnamed x2 -> x0, local copies, waits for them, and re-layouts: 0.9 us -> none
  transfers between devices with their start and end apart: 14 -> 14, of which waited for: 5 -> 5; matrix products, arithmetic and copies ran while one was open for 0% -> 0% of each run, Pallas kernels for 31% -> 35%
where the time goes in v3:
time: 54.4 us; the launch traced here: 54.2 us
  Pallas kernels  20.5 us (38%)
  starting transfers between devices  19.7 us (36%)
  waiting for transfers between devices  11 us (20%)
  other arithmetic  1.94 us (4%)
  local copies, waits for them, and re-layouts  0.85 us (2%)
    ppermute x14, starting transfers between devices, moved(): return lax.ppermute(value, ('ka', 'mu'), pairs)  19.7 us
    ppermute x14, waiting for transfers between devices, moved(): return lax.ppermute(value, ('ka', 'mu'), pairs)  11 us
    pallas_call x2, Pallas kernels, fold(): pl.pallas_call(functools.partial(fold_kernel, count, used, later), out_sh...  10.1 us
    pallas_call x1, Pallas kernels, local(): first(info, *vec_parts, *con_parts[1:], bundle_home, bundle[NEAR], screened)  8.91 us
    pallas_call x1, Pallas kernels, local(): pl.pallas_call(functools.partial(result_kernel, count), out_shape=[jax.Sh...  1.55 us
  transfers between devices with their start and end apart: 14, of which 5 were waited for; matrix products, arithmetic and copies ran while one was open for 0% of the time, Pallas kernels for 35%

profile of v3, /device:TPU:0, one launch (start us, length us, event | category | flops | bytes accessed | tf_op | source)
XLA Modules:
  0.0 54.2 jit_solution(763450594627637829)
XLA Ops:
  0.0 0.8 %convert_reduce_fusion = bf16[3,2048]{1,0:T(4,128)(2,1)S(1)} fusion(f32[3,1,2048]{2,1,0:T(1,128)} %param.5), kind=kLoop, calls=%fused_computation.14 | loop fusion | flops 6144 | bytes 36864 | tf_op jit(solution)/shard_map/convert_element_type | solution.py:170
  0.8 0.1 reshape.9.refs_0_
  0.9 1.0 %pad_maximum_fusion.1.refs_3_ = bf16[128,1024]{1,0:T(8,128)(2,1)S(1)} fusion(bf16[64,1024]{1,0:T(8,128)(2,1)} %bitcast.28, bf16[64,1024]{1,0:T(8,128)(2,1)} %bitcast.27), kind=kLoop, calls=%fused_computation.1 | loop fusion | flops 524288 | bytes 524288 | tf_op jit(solution)/shard_map/concatenate | solution.py:172
  1.9 6.1 %collective-permute-start.3 = (bf16[128,1024]{1,0:T(8,128)(2,1)S(1)}, bf16[128,1024]{1,0:T(8,128)(2,1)S(1)}, u32[]{:S(2)}, u32[]{:S(2)}) collective-permute-start(bf16[128,1024]{1,0:T(8,128)(2,1)S(1)} %pad_maximum_fusion.1.refs_3_), channel_id=1, source_target_pairs={{0,28},{1,29},{2,6},{3,7},{4,0},{5,1},{6,10},{7,11},{8,4},{9,5},{1... | collective-permute-start | bytes 786440 | tf_op jit(solution)/shard_map/ppermute | solution.py:138
  8.0 0.0 collective-permute-start.4
  8.0 0.0 collective-permute-start.2
  8.0 1.5 %collective-permute-start.1 = (bf16[64,1024]{1,0:T(8,128)(2,1)}, bf16[64,1024]{1,0:T(8,128)(2,1)S(1)}, u32[]{:S(2)}, u32[]{:S(2)}) collective-permute-start(bf16[64,1024]{1,0:T(8,128)(2,1)} %bitcast.29), channel_id=1, source_target_pairs={{0,1},{1,0},{2,3},{3,2},{4,5},{5,4},{6,7},{7,6},{8,9},{9,8},{10,11... | collective-permute-start | bytes 393224 | tf_op jit(solution)/shard_map/ppermute | solution.py:138
  9.5 0.5 collective-permute-start
  10.0 0.1 pad_add_fusion.info
  10.1 4.3 %collective-permute-done.1.refs_2_ = bf16[64,1024]{1,0:T(8,128)(2,1)S(1)} collective-permute-done((bf16[64,1024]{1,0:T(8,128)(2,1)}, bf16[64,1024]{1,0:T(8,128)(2,1)S(1)}, u32[]{:S(2)}, u32[]{:S(2)}) %collective-permute-start.1) | collective-permute-done | bytes 131104 | tf_op jit(solution)/shard_map/ppermute | solution.py:138
  14.3 0.0 collective-permute-start.6
  14.4 0.0 collective-permute-done.3.refs_1_.refs_6_
  14.4 5.4 %collective-permute-start.7 = (bf16[64,1024]{1,0:T(8,128)(2,1)S(1)}, bf16[64,1024]{1,0:T(8,128)(2,1)S(1)}, u32[]{:S(2)}, u32[]{:S(2)}) collective-permute-start(bf16[64,1024]{1,0:T(8,128)(2,1)S(1)} %slice.42), channel_id=1, source_target_pairs={{0,1},{1,0},{2,3},{3,2},{4,5},{5,4},{6,7},{7,6},{8,9},{9,8},{10,11... | collective-permute-start | bytes 393224 | tf_op jit(solution)/shard_map/ppermute | solution.py:138
  19.7 0.0 collective-permute-done.4.refs_2_.refs_7_
  19.8 0.1 collective-permute-start.9
  19.9 0.0 collective-permute-done.refs_1_
  19.9 0.1 collective-permute-start.5
  19.9 0.0 collective-permute-done.2.refs_4_
  19.9 8.9 %first.1 = (bf16[3,1024,2048]{2,1,0:T(8,128)(2,1)S(1)}, bf16[192,2048]{1,0:T(8,128)(2,1)S(1)}, bf16[1024,2048]{1,0:T(8,128)(2,1)S(1)}, bf16[1024,2048]{1,0:T(8,128)(2,1)S(1)}) custom-call(s32[5]{0:T(128)S(1)} %pad_add_fusion.info, bf16[3,32,64]{2,1,0:T(8,128)(2,1)S(1)} %reshape.9.refs_0_, bf16[3,32,64]{2,1,0:T(8,128)(2,1)S(1)} %collective-permute-done.refs_1_, ...), custom_call_target="tpu_custom_call" | custom-call | flops 6442450944 | bytes 4194304 | tf_op jit(solution)/shard_map/first/pallas_call | solution.py:204
  28.9 7.2 %shard_map.46 = (bf16[3,1024,2048]{2,1,0:T(8,128)(2,1)S(1)}, bf16[192,2048]{1,0:T(8,128)(2,1)S(1)}, bf16[192,2048]{1,0:T(8,128)(2,1)S(1)}, bf16[1024,2048]{1,0:T(8,128)(2,1)S(1)}) custom-call(s32[5]{0:T(128)S(1)} %pad_add_fusion.info, bf16[3,1024,2048]{2,1,0:T(8,128)(2,1)S(1)} %get-tuple-element.21.refs_0_, ...), custom_call_target="tpu_custom_call", output_to_operand_aliasing={{0}: (1, {})} | custom-call | flops 6442450944 | bytes 8388608 | tf_op jit(solution)/shard_map/pallas_call | solution.py:211
  36.1 0.0 collective-permute-done.7.refs_10_
  36.1 0.6 %collective-permute-start.8 = (bf16[64,1024]{1,0:T(8,128)(2,1)S(1)}, bf16[64,1024]{1,0:T(8,128)(2,1)S(1)}, u32[]{:S(2)}, u32[]{:S(2)}) collective-permute-start(bf16[64,1024]{1,0:T(8,128)(2,1)S(1)} %collective-permute-done.7.refs_10_), channel_id=1, source_target_pairs={{0,2},{1,3},{2,0},{3,1},{4,6},{5,7},{6,4},{7,5},{8,10},{9,11},{10,... | collective-permute-start | bytes 393224 | tf_op jit(solution)/shard_map/ppermute | solution.py:138
  36.6 0.0 collective-permute-done.5.refs_1_.refs_5_
  36.6 2.8 %shard_map.47.refs_1_ = bf16[192,2048]{1,0:T(8,128)(2,1)S(1)} custom-call(s32[5]{0:T(128)S(1)} %pad_add_fusion.info, bf16[3,1024,2048]{2,1,0:T(8,128)(2,1)S(1)} %get-tuple-element.24.refs_0_, bf16[128,1024]{1,0:T(8,128)(2,1)S(1)} %collective-permute-done.5.refs_1_.refs_5_, bf16[1024,2048]{1,0:T(8,128)(2,1)S(1)} %get-tuple-element.25.refs_2_), custom_call_target="tpu_custom_call" | custom-call | flops 3221225472 | bytes 4194304 | tf_op jit(solution)/shard_map/pallas_call | solution.py:211
  39.5 0.0 collective-permute-done.6.refs_8_
  39.5 0.0 collective-permute-done.9.refs_11_
  39.5 0.0 collective-permute-done.8.refs_9_
  39.5 1.6 %result.1 = (f32[2,2,3,32,64]{4,3,2,1,0:T(8,128)S(1)}, f32[2,3,32,64]{3,2,1,0:T(8,128)S(1)}, f32[2,3,32,64]{3,2,1,0:T(8,128)S(1)}) custom-call(s32[5]{0:T(128)S(1)} %pad_add_fusion.info, bf16[192,2048]{1,0:T(8,128)(2,1)S(1)} %get-tuple-element.20.refs_0_, bf16[192,2048]{1,0:T(8,128)(2,1)S(1)} %shard_map.47.refs_1_, ...), custom_call_target="tpu_custom_call" | custom-call | flops 805306368 | bytes 1048576 | tf_op jit(solution)/shard_map/result/pallas_call | solution.py:236
  41.1 0.1 collective-permute-start.10
  41.2 1.4 %collective-permute-done.10 = f32[2,2,3,32,64]{4,3,2,1,0:T(8,128)S(1)} collective-permute-done((f32[2,2,3,32,64]{4,3,2,1,0:T(8,128)S(1)}, f32[2,2,3,32,64]{4,3,2,1,0:T(8,128)S(1)}, u32[]{:S(2)}, u32[]{:S(2)}) %collective-permute-start.10) | collective-permute-done | bytes 98336 | tf_op jit(solution)/shard_map/ppermute | solution.py:138
  42.7 2.0 %collective-permute-start.11 = (bf16[3,3,32,64]{3,2,1,0:T(8,128)(2,1)S(1)}, bf16[3,3,32,64]{3,2,1,0:T(8,128)(2,1)S(1)}, u32[]{:S(2)}, u32[]{:S(2)}) collective-permute-start(bf16[3,3,32,64]{3,2,1,0:T(8,128)(2,1)S(1)} %fusion.3), channel_id=1, source_target_pairs={{0,1},{1,0},{2,3},{3,2},{4,5},{5,4},{6,7},{7,6},{8,9},{9,8},{10,11... | collective-permute-start | bytes 110600 | tf_op jit(solution)/shard_map/ppermute | solution.py:138
  44.7 2.6 %collective-permute-done.11 = bf16[3,3,32,64]{3,2,1,0:T(8,128)(2,1)S(1)} collective-permute-done((bf16[3,3,32,64]{3,2,1,0:T(8,128)(2,1)S(1)}, bf16[3,3,32,64]{3,2,1,0:T(8,128)(2,1)S(1)}, u32[]{:S(2)}, u32[]{:S(2)}) %collective-permute-start.11) | collective-permute-done | bytes 36896 | tf_op jit(solution)/shard_map/ppermute | solution.py:138
  47.3 3.2 %collective-permute-start.12 = (bf16[2,3,32,64]{3,2,1,0:T(8,128)(2,1)S(1)}, bf16[2,3,32,64]{3,2,1,0:T(8,128)(2,1)S(1)}, u32[]{:S(2)}, u32[]{:S(2)}) collective-permute-start(bf16[2,3,32,64]{3,2,1,0:T(8,128)(2,1)S(1)} %slice.71), channel_id=1, source_target_pairs={{0,28},{1,29},{2,6},{3,7},{4,0},{5,1},{6,10},{7,11},{8,4},{9,5},{1... | collective-permute-start | bytes 73736 | tf_op jit(solution)/shard_map/ppermute | solution.py:138
  50.5 1.8 %collective-permute-done.12 = bf16[2,3,32,64]{3,2,1,0:T(8,128)(2,1)S(1)} collective-permute-done((bf16[2,3,32,64]{3,2,1,0:T(8,128)(2,1)S(1)}, bf16[2,3,32,64]{3,2,1,0:T(8,128)(2,1)S(1)}, u32[]{:S(2)}, u32[]{:S(2)}) %collective-permute-start.12) | collective-permute-done | bytes 24608 | tf_op jit(solution)/shard_map/ppermute | solution.py:138
  52.2 0.2 collective-permute-start.13
  52.5 1.0 %collective-permute-done.13 = bf16[3,32,64]{2,1,0:T(8,128)(2,1)S(1)} collective-permute-done((bf16[3,32,64]{2,1,0:T(8,128)(2,1)S(1)}, bf16[3,32,64]{2,1,0:T(8,128)(2,1)S(1)}, u32[]{:S(2)}, u32[]{:S(2)}) %collective-permute-start.13) | collective-permute-done | bytes 12320 | tf_op jit(solution)/shard_map/ppermute | solution.py:138
  53.5 0.7 %reshape.11 = f32[3,1,2048]{2,1,0:T(1,128)} reshape(f32[3,32,64]{2,1,0:T(8,128)S(1)} %fusion.5) | data formatting | bytes 49152 | tf_op jit(solution)/shard_map/reshape | solution.py:263
  (11 shorter events, 0.1 us)
Async XLA Ops:
  1.9 12.5 %collective-permute-start.3 = (bf16[128,1024]{1,0:T(8,128)(2,1)S(1)}, bf16[128,1024]{1,0:T(8,128)(2,1)S(1)}, u32[]{:S(2)}, u32[]{:S(2)}) collective-permute-start(bf16[128,1024]{1,0:T(8,128)(2,1)S(1)} %pad_maximum_fusion.1.refs_3_), channel_id=1, source_target_pairs={{0,28},{1,29},{2,6},{3,7},{4,0},{5,1},{6,10},{7,11},{8,4},{9,5},{1... | collective-permute-start | bytes 786440 | tf_op jit(solution)/shard_map/ppermute | solution.py:138
  8.0 11.8 %collective-permute-start.4 = (bf16[128,1024]{1,0:T(8,128)(2,1)S(1)}, bf16[128,1024]{1,0:T(8,128)(2,1)S(1)}, u32[]{:S(2)}, u32[]{:S(2)}) collective-permute-start(bf16[128,1024]{1,0:T(8,128)(2,1)S(1)} %pad_maximum_fusion.1.refs_3_), channel_id=1, source_target_pairs={{0,4},{1,5},{2,30},{3,31},{4,8},{5,9},{6,2},{7,3},{8,12},{9,13},{1... | collective-permute-start | bytes 786440 | tf_op jit(solution)/shard_map/ppermute | solution.py:138
  8.0 12.0 %collective-permute-start.2 = (bf16[128,1024]{1,0:T(8,128)(2,1)S(1)}, bf16[128,1024]{1,0:T(8,128)(2,1)S(1)}, u32[]{:S(2)}, u32[]{:S(2)}) collective-permute-start(bf16[128,1024]{1,0:T(8,128)(2,1)S(1)} %pad_maximum_fusion.1.refs_3_), channel_id=1, source_target_pairs={{0,2},{1,3},{2,0},{3,1},{4,6},{5,7},{6,4},{7,5},{8,10},{9,11},{10,... | collective-permute-start | bytes 786440 | tf_op jit(solution)/shard_map/ppermute | solution.py:138
  8.0 6.4 %collective-permute-start.1 = (bf16[64,1024]{1,0:T(8,128)(2,1)}, bf16[64,1024]{1,0:T(8,128)(2,1)S(1)}, u32[]{:S(2)}, u32[]{:S(2)}) collective-permute-start(bf16[64,1024]{1,0:T(8,128)(2,1)} %bitcast.29), channel_id=1, source_target_pairs={{0,1},{1,0},{2,3},{3,2},{4,5},{5,4},{6,7},{7,6},{8,9},{9,8},{10,11... | collective-permute-start | bytes 393224 | tf_op jit(solution)/shard_map/ppermute | solution.py:138
  9.5 10.4 %collective-permute-start = (bf16[3,32,64]{2,1,0:T(8,128)(2,1)S(1)}, bf16[3,32,64]{2,1,0:T(8,128)(2,1)S(1)}, u32[]{:S(2)}, u32[]{:S(2)}) collective-permute-start(bf16[3,32,64]{2,1,0:T(8,128)(2,1)S(1)} %reshape.9.refs_0_), channel_id=1, source_target_pairs={{0,1},{1,0},{2,3},{3,2},{4,5},{5,4},{6,7},{7,6},{8,9},{9,8},{10,11... | collective-permute-start | bytes 36872 | tf_op jit(solution)/shard_map/ppermute | solution.py:138
  14.3 25.2 %collective-permute-start.6 = (bf16[64,1024]{1,0:T(8,128)(2,1)S(1)}, bf16[64,1024]{1,0:T(8,128)(2,1)S(1)}, u32[]{:S(2)}, u32[]{:S(2)}) collective-permute-start(bf16[64,1024]{1,0:T(8,128)(2,1)S(1)} %collective-permute-done.1.refs_2_), channel_id=1, source_target_pairs={{0,2},{1,3},{2,0},{3,1},{4,6},{5,7},{6,4},{7,5},{8,10},{9,11},{10,... | collective-permute-start | bytes 393224 | tf_op jit(solution)/shard_map/ppermute | solution.py:138
  14.4 21.7 %collective-permute-start.7 = (bf16[64,1024]{1,0:T(8,128)(2,1)S(1)}, bf16[64,1024]{1,0:T(8,128)(2,1)S(1)}, u32[]{:S(2)}, u32[]{:S(2)}) collective-permute-start(bf16[64,1024]{1,0:T(8,128)(2,1)S(1)} %slice.42), channel_id=1, source_target_pairs={{0,1},{1,0},{2,3},{3,2},{4,5},{5,4},{6,7},{7,6},{8,9},{9,8},{10,11... | collective-permute-start | bytes 393224 | tf_op jit(solution)/shard_map/ppermute | solution.py:138
  19.8 19.7 %collective-permute-start.9 = (bf16[64,1024]{1,0:T(8,128)(2,1)S(1)}, bf16[64,1024]{1,0:T(8,128)(2,1)S(1)}, u32[]{:S(2)}, u32[]{:S(2)}) collective-permute-start(bf16[64,1024]{1,0:T(8,128)(2,1)S(1)} %slice.43), channel_id=1, source_target_pairs={{0,1},{1,0},{2,3},{3,2},{4,5},{5,4},{6,7},{7,6},{8,9},{9,8},{10,11... | collective-permute-start | bytes 393224 | tf_op jit(solution)/shard_map/ppermute | solution.py:138
  19.9 16.8 %collective-permute-start.5 = (bf16[128,1024]{1,0:T(8,128)(2,1)S(1)}, bf16[128,1024]{1,0:T(8,128)(2,1)S(1)}, u32[]{:S(2)}, u32[]{:S(2)}) collective-permute-start(bf16[128,1024]{1,0:T(8,128)(2,1)S(1)} %collective-permute-done.3.refs_1_.refs_6_), channel_id=1, source_target_pairs={{0,2},{1,3},{2,0},{3,1},{4,6},{5,7},{6,4},{7,5},{8,10},{9,11},{10,... | collective-permute-start | bytes 786440 | tf_op jit(solution)/shard_map/ppermute | solution.py:138
  36.1 3.4 %collective-permute-start.8 = (bf16[64,1024]{1,0:T(8,128)(2,1)S(1)}, bf16[64,1024]{1,0:T(8,128)(2,1)S(1)}, u32[]{:S(2)}, u32[]{:S(2)}) collective-permute-start(bf16[64,1024]{1,0:T(8,128)(2,1)S(1)} %collective-permute-done.7.refs_10_), channel_id=1, source_target_pairs={{0,2},{1,3},{2,0},{3,1},{4,6},{5,7},{6,4},{7,5},{8,10},{9,11},{10,... | collective-permute-start | bytes 393224 | tf_op jit(solution)/shard_map/ppermute | solution.py:138
  41.1 1.5 %collective-permute-start.10 = (f32[2,2,3,32,64]{4,3,2,1,0:T(8,128)S(1)}, f32[2,2,3,32,64]{4,3,2,1,0:T(8,128)S(1)}, u32[]{:S(2)}, u32[]{:S(2)}) collective-permute-start(f32[2,2,3,32,64]{4,3,2,1,0:T(8,128)S(1)} %get-tuple-element.28), channel_id=1, source_target_pairs={{0,2},{1,3},{2,0},{3,1},{4,6},{5,7},{6,4},{7,5},{8,10},{9,11},{10,... | collective-permute-start | bytes 294920 | tf_op jit(solution)/shard_map/ppermute | solution.py:138
  42.7 4.6 %collective-permute-start.11 = (bf16[3,3,32,64]{3,2,1,0:T(8,128)(2,1)S(1)}, bf16[3,3,32,64]{3,2,1,0:T(8,128)(2,1)S(1)}, u32[]{:S(2)}, u32[]{:S(2)}) collective-permute-start(bf16[3,3,32,64]{3,2,1,0:T(8,128)(2,1)S(1)} %fusion.3), channel_id=1, source_target_pairs={{0,1},{1,0},{2,3},{3,2},{4,5},{5,4},{6,7},{7,6},{8,9},{9,8},{10,11... | collective-permute-start | bytes 110600 | tf_op jit(solution)/shard_map/ppermute | solution.py:138
  47.3 5.0 %collective-permute-start.12 = (bf16[2,3,32,64]{3,2,1,0:T(8,128)(2,1)S(1)}, bf16[2,3,32,64]{3,2,1,0:T(8,128)(2,1)S(1)}, u32[]{:S(2)}, u32[]{:S(2)}) collective-permute-start(bf16[2,3,32,64]{3,2,1,0:T(8,128)(2,1)S(1)} %slice.71), channel_id=1, source_target_pairs={{0,28},{1,29},{2,6},{3,7},{4,0},{5,1},{6,10},{7,11},{8,4},{9,5},{1... | collective-permute-start | bytes 73736 | tf_op jit(solution)/shard_map/ppermute | solution.py:138
  52.2 1.2 %collective-permute-start.13 = (bf16[3,32,64]{2,1,0:T(8,128)(2,1)S(1)}, bf16[3,32,64]{2,1,0:T(8,128)(2,1)S(1)}, u32[]{:S(2)}, u32[]{:S(2)}) collective-permute-start(bf16[3,32,64]{2,1,0:T(8,128)(2,1)S(1)} %slice_bitcast_fusion.2), channel_id=1, source_target_pairs={{0,2},{1,3},{2,0},{3,1},{4,6},{5,7},{6,4},{7,5},{8,10},{9,11},{10,... | collective-permute-start | bytes 36872 | tf_op jit(solution)/shard_map/ppermute | solution.py:138

commit v4 on v3

--- a/solution.py
+++ b/solution.py
@@ -101,15 +101,15 @@
             copy.wait()
 
 
-def result_kernel(count, info, *refs):
-    foldeds, bundles = refs[:4], refs[4:8]
-    others = refs[8 : 8 + 4 * (count - 1)]
-    near, far, behind, work = refs[-4:]
-    outs = (near.at[0], far, near.at[1], behind)
-    _, vec_count, rows, _ = far.shape
+def result_kernel(count, used, info, *refs):
+    foldeds, bundles = refs[:used], refs[used : 2 * used]
+    others = refs[2 * used : 2 * used + used * (count - 1)]
+    arrays, work = refs[2 * used + used * (count - 1) : -1], refs[-1]
+    outs = [array.at[i] for array in arrays for i in range(array.shape[0])]
+    _, _, vec_count, rows, _ = arrays[0].shape
     valence = foldeds[0].shape[0] // vec_count
     cols = bundles[0].shape[1]
-    for i in range(4):
+    for i in range(used):
         total = contract(
             foldeds[i][:, pl.ds(0, cols)], bundles[i][pl.ds(valence, bundles[i].shape[0] - valence), :], 1, 1
         )
@@ -229,30 +229,35 @@
         return pairs, out[:used], out[used:]
 
     pairs, (folded_ahead, folded_behind), weights = fold(pairs, weights, (AHEAD, BEHIND), (FAR,))
+
+    def results(foldeds, slots, groups):
+        used = len(slots)
+        return pl.pallas_call(
+            functools.partial(result_kernel, count, used),
+            out_shape=[
+                jax.ShapeDtypeStruct((n, count, vec_count, rows, conduction), F32)
+                for n in groups
+            ],
+            in_specs=[SMEM_SPEC] + [VMEM_SPEC] * (used + used * count),
+            out_specs=[VMEM_SPEC] * len(groups),
+            scratch_shapes=[pltpu.VMEM((used, vec_count * valence, conduction), F32)],
+            compiler_params=params(10),
+            cost_estimate=pl.CostEstimate(
+                flops=used * fold_flops // 4, bytes_accessed=MIB, transcendentals=0
+            ),
+        )(
+            info,
+            *foldeds,
+            *[bundle[slot] for slot in slots],
+            *[part for slot in slots for part in others[slot]],
+        )
+
+    early = (folded_near, folded_ahead, folded_behind)
+    near, behind = results(early, (NEAR, AHEAD, BEHIND), (2, 1))
+    near = moved(near, lambda k, m: (target_of(NEAR, k), m))
     _, (folded_far,), _ = fold(pairs, weights, (FAR,), ())
-
-    result = (count, vec_count, rows, conduction)
-    order = (NEAR, FAR, AHEAD, BEHIND)
-    near, far, behind = pl.pallas_call(
-        functools.partial(result_kernel, count),
-        out_shape=[jax.ShapeDtypeStruct(s, F32) for s in ((2,) + result, result, result)],
-        in_specs=[SMEM_SPEC] + [VMEM_SPEC] * (4 + 4 * count),
-        out_specs=[VMEM_SPEC] * 3,
-        scratch_shapes=[pltpu.VMEM((4, vec_count * valence, conduction), F32)],
-        compiler_params=params(10),
-        cost_estimate=pl.CostEstimate(flops=fold_flops, bytes_accessed=MIB, transcendentals=0),
-        name="result",
-    )(
-        info,
-        folded_near,
-        folded_far,
-        folded_ahead,
-        folded_behind,
-        *[bundle[s] for s in order],
-        *[part for s in order for part in others[s]],
-    )
-    near = moved(near, lambda k, m: (target_of(NEAR, k), m))
-    shared = jnp.stack([near[0], far + near[1], behind])
+    (far,) = results((folded_far,), (FAR,), (1,))
+    shared = jnp.stack([near[0], far[0] + near[1], behind[0]])
     summed = shared[:, 0]
     for part in range(1, count):
         sent = shared[:, part].astype(BF16)

time: 54.4 us -> 54.1 us (level)
  waiting for transfers between devices: 11 us -> 9.77 us
  Pallas kernels: 20.5 us -> 21.2 us
    ppermute x14, waiting for transfers between devices: 11 us -> 9.77 us  [moved(): return lax.ppermute(value, ('ka', 'mu'), pairs)]
    pallas_call x1 -> x2, Pallas kernels: 1.55 us -> 2.25 us  [results(): pl.pallas_call(functools.partial(result_kernel, count, used), out_shape=[...]
  transfers between devices with their start and end apart: 14 -> 14, of which waited for: 5 -> 4; matrix products, arithmetic and copies ran while one was open for 0% -> 0% of each run, Pallas kernels for 35% -> 39%
where the time goes in v4:
time: 54.1 us; the launch traced here: 53.9 us
  Pallas kernels  21.2 us (39%)
  starting transfers between devices  20 us (37%)
  waiting for transfers between devices  9.77 us (18%)
  other arithmetic  1.96 us (4%)
  local copies, waits for them, and re-layouts  0.84 us (2%)
    ppermute x14, starting transfers between devices, moved(): return lax.ppermute(value, ('ka', 'mu'), pairs)  20 us
    pallas_call x2, Pallas kernels, fold(): pl.pallas_call(functools.partial(fold_kernel, count, used, later), out_sh...  10.1 us
    ppermute x14, waiting for transfers between devices, moved(): return lax.ppermute(value, ('ka', 'mu'), pairs)  9.77 us
    pallas_call x1, Pallas kernels, local(): first(info, *vec_parts, *con_parts[1:], bundle_home, bundle[NEAR], screened)  8.91 us
    pallas_call x2, Pallas kernels, results(): pl.pallas_call(functools.partial(result_kernel, count, used), out_shape=[...  2.25 us
  transfers between devices with their start and end apart: 14, of which 4 were waited for; matrix products, arithmetic and copies ran while one was open for 0% of the time, Pallas kernels for 39%

profile of v4, /device:TPU:0, one launch (start us, length us, event | category | flops | bytes accessed | tf_op | source)
XLA Modules:
  0.0 53.9 jit_solution(7177834503261143758)
XLA Ops:
  0.0 0.8 %convert_reduce_fusion = bf16[3,2048]{1,0:T(4,128)(2,1)S(1)} fusion(f32[3,1,2048]{2,1,0:T(1,128)} %param.5), kind=kLoop, calls=%fused_computation.12 | loop fusion | flops 6144 | bytes 36864 | tf_op jit(solution)/shard_map/convert_element_type | solution.py:170
  0.8 0.1 reshape.9.refs_0_
  0.9 1.0 %pad_maximum_fusion.1.refs_3_ = bf16[128,1024]{1,0:T(8,128)(2,1)S(1)} fusion(bf16[64,1024]{1,0:T(8,128)(2,1)} %bitcast.18, bf16[64,1024]{1,0:T(8,128)(2,1)} %bitcast.17), kind=kLoop, calls=%fused_computation.1 | loop fusion | flops 524288 | bytes 524288 | tf_op jit(solution)/shard_map/concatenate | solution.py:172
  1.9 6.1 %collective-permute-start.3 = (bf16[128,1024]{1,0:T(8,128)(2,1)S(1)}, bf16[128,1024]{1,0:T(8,128)(2,1)S(1)}, u32[]{:S(2)}, u32[]{:S(2)}) collective-permute-start(bf16[128,1024]{1,0:T(8,128)(2,1)S(1)} %pad_maximum_fusion.1.refs_3_), channel_id=1, source_target_pairs={{0,28},{1,29},{2,6},{3,7},{4,0},{5,1},{6,10},{7,11},{8,4},{9,5},{1... | collective-permute-start | bytes 786440 | tf_op jit(solution)/shard_map/ppermute | solution.py:138
  8.0 0.0 collective-permute-start.4
  8.0 0.0 collective-permute-start.2
  8.0 1.5 %collective-permute-start.1 = (bf16[64,1024]{1,0:T(8,128)(2,1)}, bf16[64,1024]{1,0:T(8,128)(2,1)S(1)}, u32[]{:S(2)}, u32[]{:S(2)}) collective-permute-start(bf16[64,1024]{1,0:T(8,128)(2,1)} %bitcast.19), channel_id=1, source_target_pairs={{0,1},{1,0},{2,3},{3,2},{4,5},{5,4},{6,7},{7,6},{8,9},{9,8},{10,11... | collective-permute-start | bytes 393224 | tf_op jit(solution)/shard_map/ppermute | solution.py:138
  9.5 0.5 collective-permute-start
  10.0 0.1 pad_add_fusion.info
  10.1 4.3 %collective-permute-done.1.refs_2_ = bf16[64,1024]{1,0:T(8,128)(2,1)S(1)} collective-permute-done((bf16[64,1024]{1,0:T(8,128)(2,1)}, bf16[64,1024]{1,0:T(8,128)(2,1)S(1)}, u32[]{:S(2)}, u32[]{:S(2)}) %collective-permute-start.1) | collective-permute-done | bytes 131104 | tf_op jit(solution)/shard_map/ppermute | solution.py:138
  14.3 0.0 collective-permute-start.5
  14.4 0.0 collective-permute-done.3.refs_1_.refs_4_
  14.4 5.4 %collective-permute-start.6 = (bf16[64,1024]{1,0:T(8,128)(2,1)S(1)}, bf16[64,1024]{1,0:T(8,128)(2,1)S(1)}, u32[]{:S(2)}, u32[]{:S(2)}) collective-permute-start(bf16[64,1024]{1,0:T(8,128)(2,1)S(1)} %slice.42), channel_id=1, source_target_pairs={{0,1},{1,0},{2,3},{3,2},{4,5},{5,4},{6,7},{7,6},{8,9},{9,8},{10,11... | collective-permute-start | bytes 393224 | tf_op jit(solution)/shard_map/ppermute | solution.py:138
  19.7 0.0 collective-permute-done.4.refs_2_.refs_5_
  19.8 0.1 collective-permute-start.7
  19.9 0.0 collective-permute-done.refs_1_
  19.9 0.1 collective-permute-start.9
  19.9 0.0 collective-permute-done.2.refs_4_.refs_3_
  19.9 8.9 %first.1 = (bf16[3,1024,2048]{2,1,0:T(8,128)(2,1)S(1)}, bf16[192,2048]{1,0:T(8,128)(2,1)S(1)}, bf16[1024,2048]{1,0:T(8,128)(2,1)S(1)}, bf16[1024,2048]{1,0:T(8,128)(2,1)S(1)}) custom-call(s32[5]{0:T(128)S(1)} %pad_add_fusion.info, bf16[3,32,64]{2,1,0:T(8,128)(2,1)S(1)} %reshape.9.refs_0_, bf16[3,32,64]{2,1,0:T(8,128)(2,1)S(1)} %collective-permute-done.refs_1_, ...), custom_call_target="tpu_custom_call" | custom-call | flops 6442450944 | bytes 4194304 | tf_op jit(solution)/shard_map/first/pallas_call | solution.py:204
  28.9 7.2 %shard_map.46 = (bf16[3,1024,2048]{2,1,0:T(8,128)(2,1)S(1)}, bf16[192,2048]{1,0:T(8,128)(2,1)S(1)}, bf16[192,2048]{1,0:T(8,128)(2,1)S(1)}, bf16[1024,2048]{1,0:T(8,128)(2,1)S(1)}) custom-call(s32[5]{0:T(128)S(1)} %pad_add_fusion.info, bf16[3,1024,2048]{2,1,0:T(8,128)(2,1)S(1)} %get-tuple-element.20.refs_0_, ...), custom_call_target="tpu_custom_call", output_to_operand_aliasing={{0}: (1, {})} | custom-call | flops 6442450944 | bytes 8388608 | tf_op jit(solution)/shard_map/pallas_call | solution.py:211
  36.1 0.0 collective-permute-done.5.refs_6_
  36.1 0.0 collective-permute-done.6.refs_7_
  36.1 0.0 collective-permute-done.7.refs_8_
  36.1 1.3 %shard_map.47 = (f32[2,2,3,32,64]{4,3,2,1,0:T(8,128)S(1)}, f32[1,2,3,32,64]{4,3,2,1,0:T(8,128)S(1)}) custom-call(s32[5]{0:T(128)S(1)} %pad_add_fusion.info, bf16[192,2048]{1,0:T(8,128)(2,1)S(1)} %get-tuple-element.19.refs_0_, bf16[192,2048]{1,0:T(8,128)(2,1)S(1)} %get-tuple-element.23.refs_1_, bf16[192,2048]{1,0:T(8,128)(2,1)S(1)} %get-tuple-element.24.refs_2_, ...), custom_call_target="tpu_custom_call" | custom-call | flops 603979776 | bytes 1048576 | tf_op jit(solution)/shard_map/pallas_call | solution.py:235
  37.5 0.6 %collective-permute-start.8 = (f32[2,2,3,32,64]{4,3,2,1,0:T(8,128)S(1)}, f32[2,2,3,32,64]{4,3,2,1,0:T(8,128)S(1)}, u32[]{:S(2)}, u32[]{:S(2)}) collective-permute-start(f32[2,2,3,32,64]{4,3,2,1,0:T(8,128)S(1)} %get-tuple-element.25), channel_id=1, source_target_pairs={{0,2},{1,3},{2,0},{3,1},{4,6},{5,7},{6,4},{7,5},{8,10},{9,11},{10,... | collective-permute-start | bytes 294920 | tf_op jit(solution)/shard_map/ppermute | solution.py:138
  38.0 0.1 collective-permute-start.10
  38.1 0.0 collective-permute-done.9.refs_1_
  38.1 2.8 %shard_map.48.refs_0_ = bf16[192,2048]{1,0:T(8,128)(2,1)S(1)} custom-call(s32[5]{0:T(128)S(1)} %pad_add_fusion.info, bf16[3,1024,2048]{2,1,0:T(8,128)(2,1)S(1)} %get-tuple-element.26.refs_0_, bf16[128,1024]{1,0:T(8,128)(2,1)S(1)} %collective-permute-done.9.refs_1_, bf16[1024,2048]{1,0:T(8,128)(2,1)S(1)} %get-tuple-element.27.refs_2_), custom_call_target="tpu_custom_call" | custom-call | flops 3221225472 | bytes 4194304 | tf_op jit(solution)/shard_map/pallas_call | solution.py:211
  40.9 0.0 collective-permute-done.10.refs_2_
  41.0 0.9 %shard_map.49 = f32[1,2,3,32,64]{4,3,2,1,0:T(8,128)S(1)} custom-call(s32[5]{0:T(128)S(1)} %pad_add_fusion.info, bf16[192,2048]{1,0:T(8,128)(2,1)S(1)} %shard_map.48.refs_0_, bf16[128,1024]{1,0:T(8,128)(2,1)S(1)} %collective-permute-done.9.refs_1_, bf16[64,1024]{1,0:T(8,128)(2,1)S(1)} %collective-permute-done.10.refs_2_), custom_call_target="tpu_custom_call" | custom-call | flops 201326592 | bytes 1048576 | tf_op jit(solution)/shard_map/pallas_call | solution.py:235
  41.9 0.0 collective-permute-done.8
  42.0 2.0 %collective-permute-start.11 = (bf16[3,3,32,64]{3,2,1,0:T(8,128)(2,1)S(1)}, bf16[3,3,32,64]{3,2,1,0:T(8,128)(2,1)S(1)}, u32[]{:S(2)}, u32[]{:S(2)}) collective-permute-start(bf16[3,3,32,64]{3,2,1,0:T(8,128)(2,1)S(1)} %fusion.1), channel_id=1, source_target_pairs={{0,1},{1,0},{2,3},{3,2},{4,5},{5,4},{6,7},{7,6},{8,9},{9,8},{10,11... | collective-permute-start | bytes 110600 | tf_op jit(solution)/shard_map/ppermute | solution.py:138
  44.0 2.9 %collective-permute-done.11 = bf16[3,3,32,64]{3,2,1,0:T(8,128)(2,1)S(1)} collective-permute-done((bf16[3,3,32,64]{3,2,1,0:T(8,128)(2,1)S(1)}, bf16[3,3,32,64]{3,2,1,0:T(8,128)(2,1)S(1)}, u32[]{:S(2)}, u32[]{:S(2)}) %collective-permute-start.11) | collective-permute-done | bytes 36896 | tf_op jit(solution)/shard_map/ppermute | solution.py:138
  46.9 3.1 %collective-permute-start.12 = (bf16[2,3,32,64]{3,2,1,0:T(8,128)(2,1)S(1)}, bf16[2,3,32,64]{3,2,1,0:T(8,128)(2,1)S(1)}, u32[]{:S(2)}, u32[]{:S(2)}) collective-permute-start(bf16[2,3,32,64]{3,2,1,0:T(8,128)(2,1)S(1)} %slice.67), channel_id=1, source_target_pairs={{0,28},{1,29},{2,6},{3,7},{4,0},{5,1},{6,10},{7,11},{8,4},{9,5},{1... | collective-permute-start | bytes 73736 | tf_op jit(solution)/shard_map/ppermute | solution.py:138
  50.0 1.8 %collective-permute-done.12 = bf16[2,3,32,64]{3,2,1,0:T(8,128)(2,1)S(1)} collective-permute-done((bf16[2,3,32,64]{3,2,1,0:T(8,128)(2,1)S(1)}, bf16[2,3,32,64]{3,2,1,0:T(8,128)(2,1)S(1)}, u32[]{:S(2)}, u32[]{:S(2)}) %collective-permute-start.12) | collective-permute-done | bytes 24608 | tf_op jit(solution)/shard_map/ppermute | solution.py:138
  51.8 0.6 %collective-permute-start.13 = (bf16[3,32,64]{2,1,0:T(8,128)(2,1)S(1)}, bf16[3,32,64]{2,1,0:T(8,128)(2,1)S(1)}, u32[]{:S(2)}, u32[]{:S(2)}) collective-permute-start(bf16[3,32,64]{2,1,0:T(8,128)(2,1)S(1)} %slice_bitcast_fusion.1), channel_id=1, source_target_pairs={{0,2},{1,3},{2,0},{3,1},{4,6},{5,7},{6,4},{7,5},{8,10},{9,11},{10,... | collective-permute-start | bytes 36872 | tf_op jit(solution)/shard_map/ppermute | solution.py:138
  52.3 0.8 %collective-permute-done.13 = bf16[3,32,64]{2,1,0:T(8,128)(2,1)S(1)} collective-permute-done((bf16[3,32,64]{2,1,0:T(8,128)(2,1)S(1)}, bf16[3,32,64]{2,1,0:T(8,128)(2,1)S(1)}, u32[]{:S(2)}, u32[]{:S(2)}) %collective-permute-start.13) | collective-permute-done | bytes 12320 | tf_op jit(solution)/shard_map/ppermute | solution.py:138
  53.2 0.7 %reshape.11 = f32[3,1,2048]{2,1,0:T(1,128)} reshape(f32[3,32,64]{2,1,0:T(8,128)S(1)} %fusion.3) | data formatting | bytes 49152 | tf_op jit(solution)/shard_map/reshape | solution.py:268
  (10 shorter events, 0.1 us)
Async XLA Ops:
  1.9 12.5 %collective-permute-start.3 = (bf16[128,1024]{1,0:T(8,128)(2,1)S(1)}, bf16[128,1024]{1,0:T(8,128)(2,1)S(1)}, u32[]{:S(2)}, u32[]{:S(2)}) collective-permute-start(bf16[128,1024]{1,0:T(8,128)(2,1)S(1)} %pad_maximum_fusion.1.refs_3_), channel_id=1, source_target_pairs={{0,28},{1,29},{2,6},{3,7},{4,0},{5,1},{6,10},{7,11},{8,4},{9,5},{1... | collective-permute-start | bytes 786440 | tf_op jit(solution)/shard_map/ppermute | solution.py:138
  8.0 11.8 %collective-permute-start.4 = (bf16[128,1024]{1,0:T(8,128)(2,1)S(1)}, bf16[128,1024]{1,0:T(8,128)(2,1)S(1)}, u32[]{:S(2)}, u32[]{:S(2)}) collective-permute-start(bf16[128,1024]{1,0:T(8,128)(2,1)S(1)} %pad_maximum_fusion.1.refs_3_), channel_id=1, source_target_pairs={{0,4},{1,5},{2,30},{3,31},{4,8},{5,9},{6,2},{7,3},{8,12},{9,13},{1... | collective-permute-start | bytes 786440 | tf_op jit(solution)/shard_map/ppermute | solution.py:138
  8.0 12.0 %collective-permute-start.2 = (bf16[128,1024]{1,0:T(8,128)(2,1)S(1)}, bf16[128,1024]{1,0:T(8,128)(2,1)S(1)}, u32[]{:S(2)}, u32[]{:S(2)}) collective-permute-start(bf16[128,1024]{1,0:T(8,128)(2,1)S(1)} %pad_maximum_fusion.1.refs_3_), channel_id=1, source_target_pairs={{0,2},{1,3},{2,0},{3,1},{4,6},{5,7},{6,4},{7,5},{8,10},{9,11},{10,... | collective-permute-start | bytes 786440 | tf_op jit(solution)/shard_map/ppermute | solution.py:138
  8.0 6.4 %collective-permute-start.1 = (bf16[64,1024]{1,0:T(8,128)(2,1)}, bf16[64,1024]{1,0:T(8,128)(2,1)S(1)}, u32[]{:S(2)}, u32[]{:S(2)}) collective-permute-start(bf16[64,1024]{1,0:T(8,128)(2,1)} %bitcast.19), channel_id=1, source_target_pairs={{0,1},{1,0},{2,3},{3,2},{4,5},{5,4},{6,7},{7,6},{8,9},{9,8},{10,11... | collective-permute-start | bytes 393224 | tf_op jit(solution)/shard_map/ppermute | solution.py:138
  9.5 10.4 %collective-permute-start = (bf16[3,32,64]{2,1,0:T(8,128)(2,1)S(1)}, bf16[3,32,64]{2,1,0:T(8,128)(2,1)S(1)}, u32[]{:S(2)}, u32[]{:S(2)}) collective-permute-start(bf16[3,32,64]{2,1,0:T(8,128)(2,1)S(1)} %reshape.9.refs_0_), channel_id=1, source_target_pairs={{0,1},{1,0},{2,3},{3,2},{4,5},{5,4},{6,7},{7,6},{8,9},{9,8},{10,11... | collective-permute-start | bytes 36872 | tf_op jit(solution)/shard_map/ppermute | solution.py:138
  14.3 21.7 %collective-permute-start.5 = (bf16[64,1024]{1,0:T(8,128)(2,1)S(1)}, bf16[64,1024]{1,0:T(8,128)(2,1)S(1)}, u32[]{:S(2)}, u32[]{:S(2)}) collective-permute-start(bf16[64,1024]{1,0:T(8,128)(2,1)S(1)} %collective-permute-done.1.refs_2_), channel_id=1, source_target_pairs={{0,2},{1,3},{2,0},{3,1},{4,6},{5,7},{6,4},{7,5},{8,10},{9,11},{10,... | collective-permute-start | bytes 393224 | tf_op jit(solution)/shard_map/ppermute | solution.py:138
  14.4 21.7 %collective-permute-start.6 = (bf16[64,1024]{1,0:T(8,128)(2,1)S(1)}, bf16[64,1024]{1,0:T(8,128)(2,1)S(1)}, u32[]{:S(2)}, u32[]{:S(2)}) collective-permute-start(bf16[64,1024]{1,0:T(8,128)(2,1)S(1)} %slice.42), channel_id=1, source_target_pairs={{0,1},{1,0},{2,3},{3,2},{4,5},{5,4},{6,7},{7,6},{8,9},{9,8},{10,11... | collective-permute-start | bytes 393224 | tf_op jit(solution)/shard_map/ppermute | solution.py:138
  19.8 16.3 %collective-permute-start.7 = (bf16[64,1024]{1,0:T(8,128)(2,1)S(1)}, bf16[64,1024]{1,0:T(8,128)(2,1)S(1)}, u32[]{:S(2)}, u32[]{:S(2)}) collective-permute-start(bf16[64,1024]{1,0:T(8,128)(2,1)S(1)} %slice.43), channel_id=1, source_target_pairs={{0,1},{1,0},{2,3},{3,2},{4,5},{5,4},{6,7},{7,6},{8,9},{9,8},{10,11... | collective-permute-start | bytes 393224 | tf_op jit(solution)/shard_map/ppermute | solution.py:138
  19.9 18.2 %collective-permute-start.9 = (bf16[128,1024]{1,0:T(8,128)(2,1)S(1)}, bf16[128,1024]{1,0:T(8,128)(2,1)S(1)}, u32[]{:S(2)}, u32[]{:S(2)}) collective-permute-start(bf16[128,1024]{1,0:T(8,128)(2,1)S(1)} %collective-permute-done.3.refs_1_.refs_4_), channel_id=1, source_target_pairs={{0,2},{1,3},{2,0},{3,1},{4,6},{5,7},{6,4},{7,5},{8,10},{9,11},{10,... | collective-permute-start | bytes 786440 | tf_op jit(solution)/shard_map/ppermute | solution.py:138
  37.5 4.4 %collective-permute-start.8 = (f32[2,2,3,32,64]{4,3,2,1,0:T(8,128)S(1)}, f32[2,2,3,32,64]{4,3,2,1,0:T(8,128)S(1)}, u32[]{:S(2)}, u32[]{:S(2)}) collective-permute-start(f32[2,2,3,32,64]{4,3,2,1,0:T(8,128)S(1)} %get-tuple-element.25), channel_id=1, source_target_pairs={{0,2},{1,3},{2,0},{3,1},{4,6},{5,7},{6,4},{7,5},{8,10},{9,11},{10,... | collective-permute-start | bytes 294920 | tf_op jit(solution)/shard_map/ppermute | solution.py:138
  38.0 2.9 %collective-permute-start.10 = (bf16[64,1024]{1,0:T(8,128)(2,1)S(1)}, bf16[64,1024]{1,0:T(8,128)(2,1)S(1)}, u32[]{:S(2)}, u32[]{:S(2)}) collective-permute-start(bf16[64,1024]{1,0:T(8,128)(2,1)S(1)} %collective-permute-done.6.refs_7_), channel_id=1, source_target_pairs={{0,2},{1,3},{2,0},{3,1},{4,6},{5,7},{6,4},{7,5},{8,10},{9,11},{10,... | collective-permute-start | bytes 393224 | tf_op jit(solution)/shard_map/ppermute | solution.py:138
  42.0 4.9 %collective-permute-start.11 = (bf16[3,3,32,64]{3,2,1,0:T(8,128)(2,1)S(1)}, bf16[3,3,32,64]{3,2,1,0:T(8,128)(2,1)S(1)}, u32[]{:S(2)}, u32[]{:S(2)}) collective-permute-start(bf16[3,3,32,64]{3,2,1,0:T(8,128)(2,1)S(1)} %fusion.1), channel_id=1, source_target_pairs={{0,1},{1,0},{2,3},{3,2},{4,5},{5,4},{6,7},{7,6},{8,9},{9,8},{10,11... | collective-permute-start | bytes 110600 | tf_op jit(solution)/shard_map/ppermute | solution.py:138
  46.9 4.9 %collective-permute-start.12 = (bf16[2,3,32,64]{3,2,1,0:T(8,128)(2,1)S(1)}, bf16[2,3,32,64]{3,2,1,0:T(8,128)(2,1)S(1)}, u32[]{:S(2)}, u32[]{:S(2)}) collective-permute-start(bf16[2,3,32,64]{3,2,1,0:T(8,128)(2,1)S(1)} %slice.67), channel_id=1, source_target_pairs={{0,28},{1,29},{2,6},{3,7},{4,0},{5,1},{6,10},{7,11},{8,4},{9,5},{1... | collective-permute-start | bytes 73736 | tf_op jit(solution)/shard_map/ppermute | solution.py:138
  51.8 1.4 %collective-permute-start.13 = (bf16[3,32,64]{2,1,0:T(8,128)(2,1)S(1)}, bf16[3,32,64]{2,1,0:T(8,128)(2,1)S(1)}, u32[]{:S(2)}, u32[]{:S(2)}) collective-permute-start(bf16[3,32,64]{2,1,0:T(8,128)(2,1)S(1)} %slice_bitcast_fusion.1), channel_id=1, source_target_pairs={{0,2},{1,3},{2,0},{3,1},{4,6},{5,7},{6,4},{7,5},{8,10},{9,11},{10,... | collective-permute-start | bytes 36872 | tf_op jit(solution)/shard_map/ppermute | solution.py:138
